TPU v7x, 256 devices: a whole 4x4x8 slice. The times are simulated.
256 devices in a mesh: dp: 16 (over y_lo, x, core), supp: 16 (over y_hi, z).
Axes of the slice: x: 4, y: 4 (y_hi: 2, y_lo: 2; y = y_hi * 2 + y_lo), z: 8, core: 2. Of those that a mesh axis runs over, the one named last changes fastest.
Arguments:
- support_points: float32 [16384, 256], P('supp'), may hold values from -9 to 9, as said below
- data_points: float32 [32768, 256], P('dp'), may hold values from -9 to 9, as said below
- data_weight: float32 [32768], P('dp'), may hold values from 0.5 to 5
Outputs:
- support_out: float32 [16384, 256], P('supp')
Inputs may be any that keep to these rules, and one draw needn't show every extreme that they name: `support_points`: finite points; coordinates within the stated range. `data_points`: finite points; coordinates within the stated range.
All inputs are finite; a program needn't handle non-finite values.
Results may differ from a plain program's by a relative error of at most 0.0003.
Values sent between devices are 32-bit elements; how exact they have to be, the bound alone decides.
No kernel may reach another device: no remote copies, remote signals or barrier semaphores. Data moves between devices by JAX's collectives and lax.ppermute only.
A program may use at most 64 MiB of HBM per device.

v0:
```python
import math

import jax
import jax.numpy as jnp
from jax import lax
from jax.sharding import PartitionSpec as P

D = 256
ITERS = 2
OUTER = 2


def row_logsum(scores):
    peak = lax.pmax(jnp.max(scores, axis=1), "dp")
    totals = lax.psum(jnp.sum(jnp.exp(scores - peak[:, None]), axis=1), "dp")
    return peak + jnp.log(totals)


def column_logsum(scores):
    peak = lax.pmax(jnp.max(scores, axis=0), "supp")
    totals = lax.psum(jnp.sum(jnp.exp(scores - peak[None, :]), axis=0), "supp")
    return peak + jnp.log(totals)


def body(support_points, data_points, data_weight):
    epsilon = D / 16.0
    log_support = -math.log(support_points.shape[0] * lax.axis_size("supp"))
    log_data = jnp.log(data_weight)
    data_norm = jnp.sum(data_points * data_points, axis=1)
    column_dual = jnp.zeros((data_points.shape[0],), jnp.float32)
    points = support_points
    row_dual = jnp.zeros((support_points.shape[0],), jnp.float32)
    for update_step in range(OUTER):
        inner_part = lax.dot_general(
            points,
            data_points,
            (((1,), (1,)), ((), ())),
            precision=lax.Precision.HIGHEST,
            preferred_element_type=jnp.float32,
        )
        point_norm = jnp.sum(points * points, axis=1)
        distance = point_norm[:, None] + data_norm[None, :] - 2.0 * inner_part
        for inner_step in range(ITERS):
            row_dual = epsilon * log_support - epsilon * row_logsum(
                (column_dual[None, :] - distance) / epsilon
            )
            column_dual = epsilon * log_data - epsilon * column_logsum(
                (row_dual[:, None] - distance) / epsilon
            )
        transport = jnp.exp((row_dual[:, None] + column_dual[None, :] - distance) / epsilon)
        weighted = jnp.dot(
            transport,
            data_points,
            precision=lax.Precision.HIGHEST,
            preferred_element_type=jnp.float32,
        )
        masses = jnp.sum(transport, axis=1)
        weighted, masses = lax.psum((weighted, masses), "dp")
        points = weighted / masses[:, None]
    return points


def solution(mesh):
    return jax.shard_map(
        body,
        mesh=mesh,
        in_specs=(P("supp", None), P("dp", None), P("dp")),
        out_specs=P("supp", None),
        check_vma=False,
    )
```

profile of v0, /device:TPU:1, one launch (start us, length us, event | category | flops | bytes accessed | tf_op | source)
XLA Modules:
  0.0 906.0 jit_solution(10553745792971182442)
XLA Ops:
  6.5 0.0 all-reduce.3.cloned.1.call-start
  6.5 1.4 multiply_reduce_fusion.2
  8.0 1.9 multiply_reduce_fusion
  9.9 12.0 %fusion = (f32[1024]{0:T(1024)S(1)}, f32[1024,2048]{1,0:T(8,128)}) fusion(f32[1024,256]{1,0:T(8,128)} %param.3, f32[2048,256]{1,0:T(8,128)} %param.4, f32[2048]{0:T(1024)S(1)} %multiply_reduce_fusion, f32[1024]{0:T(1024)S(1)} %multiply_reduce_fusion.2), kind=kOutput, calls=%fused_computation.20 | convolution fusion | flops 6455032832 | bytes 11550720 | tf_op jit(solution)/shard_map/dot_general | solution.py:34
  21.9 29.7 %pmax.56 = f32[1024]{0:T(1024)S(1)} all-reduce(f32[1024]{0:T(1024)S(1)} %get-tuple-element.5), channel_id=1, replica_groups=mesh['dp'=16,'supp'=16] {'dp'}, use_global_device_ids=true, to_apply=%region_3.0 | all-reduce | flops 1024 | bytes 8192 | tf_op jit(solution)/shard_map/pmax | solution.py:14
  51.6 4.5 exponential_reduce_fusion.7
  56.1 28.6 %psum.84 = f32[1024]{0:T(1024)S(1)} all-reduce(f32[1024]{0:T(1024)S(1)} %exponential_reduce_fusion.7), channel_id=1, replica_groups=mesh['dp'=16,'supp'=16] {'dp'}, use_global_device_ids=true, to_apply=%region_5.0 | all-reduce | flops 1024 | bytes 8192 | tf_op jit(solution)/shard_map/psum | solution.py:15
  84.7 0.0 copy-start.1
  84.7 4.3 fusion.1
  89.0 38.4 %pmax.57 = f32[2048]{0:T(1024)S(1)} all-reduce(f32[2048]{0:T(1024)S(1)} %fusion.1), channel_id=1, replica_groups=mesh['dp'=16,'supp'=16] {'supp'}, use_global_device_ids=true, to_apply=%region_7.0 | all-reduce | flops 2048 | bytes 16384 | tf_op jit(solution)/shard_map/pmax | solution.py:20
  127.5 4.5 exponential_reduce_fusion.6
  132.0 30.3 %psum.85 = f32[2048]{0:T(1024)S(1)} all-reduce(f32[2048]{0:T(1024)S(1)} %exponential_reduce_fusion.6), channel_id=1, replica_groups=mesh['dp'=16,'supp'=16] {'supp'}, use_global_device_ids=true, to_apply=%region_9.0 | all-reduce | flops 2048 | bytes 16384 | tf_op jit(solution)/shard_map/psum | solution.py:21
  162.3 0.0 copy-done.1
  162.3 4.3 fusion.2
  166.6 40.9 %pmax.58 = f32[1024]{0:T(1024)S(1)} all-reduce(f32[1024]{0:T(1024)S(1)} %fusion.2), channel_id=1, replica_groups=mesh['dp'=16,'supp'=16] {'dp'}, use_global_device_ids=true, to_apply=%region_11.0 | all-reduce | flops 1024 | bytes 8192 | tf_op jit(solution)/shard_map/pmax | solution.py:14
  207.5 4.5 exponential_reduce_fusion.5
  212.0 27.1 %psum.86 = f32[1024]{0:T(1024)S(1)} all-reduce(f32[1024]{0:T(1024)S(1)} %exponential_reduce_fusion.5), channel_id=1, replica_groups=mesh['dp'=16,'supp'=16] {'dp'}, use_global_device_ids=true, to_apply=%region_13.0 | all-reduce | flops 1024 | bytes 8192 | tf_op jit(solution)/shard_map/psum | solution.py:15
  239.1 0.0 copy-start
  239.1 4.4 fusion.3
  243.6 32.4 %pmax.59 = f32[2048]{0:T(1024)S(1)} all-reduce(f32[2048]{0:T(1024)S(1)} %fusion.3), channel_id=1, replica_groups=mesh['dp'=16,'supp'=16] {'supp'}, use_global_device_ids=true, to_apply=%region_15.0 | all-reduce | flops 2048 | bytes 16384 | tf_op jit(solution)/shard_map/pmax | solution.py:20
  276.0 4.5 exponential_reduce_fusion.4
  280.5 30.3 %psum.87 = f32[2048]{0:T(1024)S(1)} all-reduce(f32[2048]{0:T(1024)S(1)} %exponential_reduce_fusion.4), channel_id=1, replica_groups=mesh['dp'=16,'supp'=16] {'supp'}, use_global_device_ids=true, to_apply=%region_17.0 | all-reduce | flops 2048 | bytes 16384 | tf_op jit(solution)/shard_map/psum | solution.py:21
  310.8 0.0 copy-done
  310.8 11.0 %fusion.9 = f32[1024,256]{1,0:T(8,128)} fusion(f32[2048,256]{1,0:T(8,128)S(1)} %copy-done, f32[1024,2048]{1,0:T(8,128)} %get-tuple-element.6, f32[2048]{0:T(1024)S(1)} %multiply_subtract_fusion.4, f32[1024]{0:T(1024)S(1)} %multiply_subtract_fusion.8), kind=kOutput, calls=%fused_computation.29 | convolution fusion | flops 6448742400 | bytes 11546624 | tf_op jit(solution)/shard_map/dot_general | solution.py:51
  321.9 0.0 all-reduce.3.cloned.1.call-update
  321.9 0.0 all-reduce.5.cloned.1.call-start
  321.9 4.5 fusion.8
  326.4 41.0 %psum.89 = f32[1024]{0:T(1024)S(1)} all-reduce(f32[1024]{0:T(1024)S(1)} %fusion.8), channel_id=1, replica_groups=mesh['dp'=16,'supp'=16] {'dp'}, use_global_device_ids=true, to_apply=%region_20.0 | all-reduce | flops 1024 | bytes 8192 | tf_op jit(solution)/shard_map/psum | solution.py:58
  367.4 86.3 %all-reduce.3.cloned.1.call-done = f32[1024,256]{1,0:T(8,128)} async-done(((f32[1024,256]{1,0:T(8,128)}), f32[1024,256]{1,0:T(8,128)}) %all-reduce.3.cloned.1.call-update) | async-done | bytes 1048592 | tf_op jit(solution)/shard_map/psum | solution.py:58
  453.7 1.6 multiply_reduce_fusion.1
  455.3 11.8 %fusion.4 = (f32[1024]{0:T(1024)S(1)}, f32[1024,2048]{1,0:T(8,128)}) fusion(f32[2048]{0:T(1024)S(1)} %multiply_subtract_fusion.4, f32[2048,256]{1,0:T(8,128)S(1)} %copy-done, f32[1024,256]{1,0:T(8,128)} %all-reduce.3.cloned.1.call-done, f32[1024]{0:T(1024)S(1)} %psum.89, f32[2048]{0:T(1024)S(1)} %multiply_reduce_fusion, f32[1024]{0:T(1024)S(1)} %multiply_reduce_fusion.1), kind=kOutput, calls=%fused_computation.24 | convolution fusion | flops 6455294976 | bytes 11563008 | tf_op jit(solution)/shard_map/dot_general | solution.py:34
  467.0 27.5 %pmax.60 = f32[1024]{0:T(1024)S(1)} all-reduce(f32[1024]{0:T(1024)S(1)} %get-tuple-element.7), channel_id=1, replica_groups=mesh['dp'=16,'supp'=16] {'dp'}, use_global_device_ids=true, to_apply=%region_23.0 | all-reduce | flops 1024 | bytes 8192 | tf_op jit(solution)/shard_map/pmax | solution.py:14
  494.5 4.5 exponential_reduce_fusion.3
  499.0 30.9 %psum.90 = f32[1024]{0:T(1024)S(1)} all-reduce(f32[1024]{0:T(1024)S(1)} %exponential_reduce_fusion.3), channel_id=1, replica_groups=mesh['dp'=16,'supp'=16] {'dp'}, use_global_device_ids=true, to_apply=%region_25.0 | all-reduce | flops 1024 | bytes 8192 | tf_op jit(solution)/shard_map/psum | solution.py:15
  529.9 4.3 fusion.5
  534.2 35.4 %pmax.61 = f32[2048]{0:T(1024)S(1)} all-reduce(f32[2048]{0:T(1024)S(1)} %fusion.5), channel_id=1, replica_groups=mesh['dp'=16,'supp'=16] {'supp'}, use_global_device_ids=true, to_apply=%region_27.0 | all-reduce | flops 2048 | bytes 16384 | tf_op jit(solution)/shard_map/pmax | solution.py:20
  569.6 4.5 exponential_reduce_fusion.2
  574.1 30.2 %psum.91 = f32[2048]{0:T(1024)S(1)} all-reduce(f32[2048]{0:T(1024)S(1)} %exponential_reduce_fusion.2), channel_id=1, replica_groups=mesh['dp'=16,'supp'=16] {'supp'}, use_global_device_ids=true, to_apply=%region_29.0 | all-reduce | flops 2048 | bytes 16384 | tf_op jit(solution)/shard_map/psum | solution.py:21
  604.3 4.3 fusion.6
  608.6 41.3 %pmax.62 = f32[1024]{0:T(1024)S(1)} all-reduce(f32[1024]{0:T(1024)S(1)} %fusion.6), channel_id=1, replica_groups=mesh['dp'=16,'supp'=16] {'dp'}, use_global_device_ids=true, to_apply=%region_31.0 | all-reduce | flops 1024 | bytes 8192 | tf_op jit(solution)/shard_map/pmax | solution.py:14
  649.9 4.5 exponential_reduce_fusion.1
  654.4 27.1 %psum.92 = f32[1024]{0:T(1024)S(1)} all-reduce(f32[1024]{0:T(1024)S(1)} %exponential_reduce_fusion.1), channel_id=1, replica_groups=mesh['dp'=16,'supp'=16] {'dp'}, use_global_device_ids=true, to_apply=%region_33.0 | all-reduce | flops 1024 | bytes 8192 | tf_op jit(solution)/shard_map/psum | solution.py:15
  681.6 4.3 fusion.7
  685.9 32.2 %pmax.63 = f32[2048]{0:T(1024)S(1)} all-reduce(f32[2048]{0:T(1024)S(1)} %fusion.7), channel_id=1, replica_groups=mesh['dp'=16,'supp'=16] {'supp'}, use_global_device_ids=true, to_apply=%region_35.0 | all-reduce | flops 2048 | bytes 16384 | tf_op jit(solution)/shard_map/pmax | solution.py:20
  718.1 4.5 exponential_reduce_fusion
  722.6 30.6 %psum.93 = f32[2048]{0:T(1024)S(1)} all-reduce(f32[2048]{0:T(1024)S(1)} %exponential_reduce_fusion), channel_id=1, replica_groups=mesh['dp'=16,'supp'=16] {'supp'}, use_global_device_ids=true, to_apply=%region_37.0 | all-reduce | flops 2048 | bytes 16384 | tf_op jit(solution)/shard_map/psum | solution.py:21
  753.2 11.1 %fusion.11 = f32[1024,256]{1,0:T(8,128)} fusion(f32[2048,256]{1,0:T(8,128)S(1)} %copy-done, f32[1024,2048]{1,0:T(8,128)} %get-tuple-element.8, f32[2048]{0:T(1024)S(1)} %multiply_subtract_fusion.2, f32[1024]{0:T(1024)S(1)} %multiply_subtract_fusion.6), kind=kOutput, calls=%fused_computation.31 | convolution fusion | flops 6448742400 | bytes 11546624 | tf_op jit(solution)/shard_map/dot_general | solution.py:51
  764.2 0.0 all-reduce.5.cloned.1.call-update
  764.3 4.5 fusion.10
  768.8 40.9 %psum.95 = f32[1024]{0:T(1024)S(1)} all-reduce(f32[1024]{0:T(1024)S(1)} %fusion.10), channel_id=1, replica_groups=mesh['dp'=16,'supp'=16] {'dp'}, use_global_device_ids=true, to_apply=%region_40.0 | all-reduce | flops 1024 | bytes 8192 | tf_op jit(solution)/shard_map/psum | solution.py:58
  809.7 86.6 %all-reduce.5.cloned.1.call-done = f32[1024,256]{1,0:T(8,128)} async-done(((f32[1024,256]{1,0:T(8,128)}), f32[1024,256]{1,0:T(8,128)}) %all-reduce.5.cloned.1.call-update) | async-done | bytes 1048592 | tf_op jit(solution)/shard_map/psum | solution.py:58
  896.3 2.4 broadcast_divide_fusion
  (8 shorter events, 0.1 us)
Async XLA Ops:
  6.5 447.1 %all-reduce.3.cloned.1.call-start = ((), (), s32[]{:S(2)}) async-start(), calls=%async_computation | async-start | bytes 2097152 | tf_op jit(solution)/shard_map/psum | solution.py:58
  84.7 77.5 %copy-start.1 = (f32[2048]{0:T(1024)S(1)}, f32[2048]{0:T(1024)}, u32[]{:S(2)}) copy-start(f32[2048]{0:T(1024)} %param.5) | copy-start | bytes 24580
  239.1 71.7 %copy-start = (f32[2048,256]{1,0:T(8,128)S(1)}, f32[2048,256]{1,0:T(8,128)}, u32[]{:S(2)}) copy-start(f32[2048,256]{1,0:T(8,128)} %param.4) | copy-start | bytes 6291460
  321.9 574.4 %all-reduce.5.cloned.1.call-start = ((), (), s32[]{:S(2)}) async-start(), calls=%async_computation.1 | async-start | bytes 2097152 | tf_op jit(solution)/shard_map/psum | solution.py:58
Sparse Core Ops, SparseCore 0:
  322.0 131.6 all-reduce.2
  764.4 131.8 all-reduce.4
where the time goes:
time: 915 us; the launch traced here: 906 us
  blocking collectives  595 us (65%)
  waiting for transfers between devices  173 us (19%)
  other arithmetic  78.3 us (9%)
  matrix products  45.9 us (5%)
  between operations  14 us (2%)
    psum x2, waiting for transfers between devices, body(): weighted, masses = lax.psum((weighted, masses), 'dp')  173 us
    pmax x4, blocking collectives, row_logsum(): peak = lax.pmax(jnp.max(scores, axis=1), 'dp')  139 us
    pmax x4, blocking collectives, column_logsum(): peak = lax.pmax(jnp.max(scores, axis=0), 'supp')  138 us
    psum x4, blocking collectives, column_logsum(): totals = lax.psum(jnp.sum(jnp.exp(scores - peak[None, :]), axis=0), 'supp')  121 us
    psum x4, blocking collectives, row_logsum(): totals = lax.psum(jnp.sum(jnp.exp(scores - peak[:, None]), axis=1), 'dp')  114 us
    psum x2, blocking collectives, body(): weighted, masses = lax.psum((weighted, masses), 'dp')  81.9 us
    dot_general x2, matrix products, body(): lax.dot_general(points, data_points, (((1,), (1,)), ((), ())), precision=...  23.8 us
    dot_general x2, matrix products, body(): jnp.dot(transport, data_points, precision=lax.Precision.HIGHEST, preferre...  22.1 us
  transfers between devices with their start and end apart: 2, of which 2 were waited for; matrix products, arithmetic and copies ran while one was open for 1% of the time, Pallas kernels for 0%

commit v1 on v0

v1 whole, which is shorter than its diff:
```python
import math

import jax
import jax.numpy as jnp
from jax import lax
from jax.experimental import pallas as pl
from jax.experimental.pallas import tpu as pltpu
from jax.sharding import PartitionSpec as P

ITERS = 2
OUTER = 2
LANES = 128
ROWS = 64

F32 = jnp.float32
BF16 = jnp.bfloat16


def split(value):
    high = value.astype(BF16)
    low = (value - high.astype(F32)).astype(BF16)
    return high, low


def lane_row(block):
    return jnp.sum(block.T, axis=0, keepdims=True)


def spread_rows(vec_ref, out_ref):
    for a in range(vec_ref.shape[0]):
        block = jnp.broadcast_to(vec_ref[a : a + 1, :], (LANES, LANES))
        out_ref[a * LANES : (a + 1) * LANES, :] = block.T


def spread_cols(vec_ref, out_ref):
    for a in range(vec_ref.shape[0]):
        out_ref[:, a * LANES : (a + 1) * LANES] = jnp.broadcast_to(vec_ref[a : a + 1, :], (8, LANES))


def log_combine(parts):
    peak = jnp.max(parts, axis=0)
    return peak + jnp.log2(jnp.sum(jnp.exp2(parts - peak[None]), axis=0))


def tree(op, values):
    values = list(values)
    while len(values) > 1:
        values = [op(values[k], values[k + 1]) if k + 1 < len(values) else values[k] for k in range(0, len(values), 2)]
    return values[0]


def prepare_kernel(x_ref, high_ref, low_ref, norm_ref, *, scale):
    for a in range(x_ref.shape[0] // LANES):
        block = x_ref[a * LANES : (a + 1) * LANES, :]
        high, low = split(block)
        high_ref[a * LANES : (a + 1) * LANES, :] = high
        low_ref[a * LANES : (a + 1) * LANES, :] = low
        square = block * block
        folded = tree(jnp.add, [square[:, k : k + LANES] for k in range(0, block.shape[1], LANES)])
        norm_ref[a : a + 1, :] = lane_row(folded) * scale


def first_row_body(points_ref, high_ref, low_ref, shift_ref, scores_ref, norm_ref, out_ref, cols_ref, peak_ref, total_ref, scale):
    m, n = scores_ref.shape
    tiles = n // LANES
    high, low = split(points_ref[...] * (2.0 * scale))
    nt = (((1,), (1,)), ((), ()))
    for k in range(0, n, 256):
        xh = high_ref[k : k + 256, :]
        xl = low_ref[k : k + 256, :]
        acc = lax.dot_general(high, xh, nt, preferred_element_type=F32)
        acc = acc + lax.dot_general(high, xl, nt, preferred_element_type=F32)
        acc = acc + lax.dot_general(low, xh, nt, preferred_element_type=F32)
        scores_ref[:, k : k + 256] = acc
    spread_cols(shift_ref, cols_ref)

    def step(b, carry):
        for half in range(2):
            rows = pl.ds(pl.multiple_of(b * 16 + half * 8, 8), 8)
            q = [scores_ref[rows, t * LANES : (t + 1) * LANES] + cols_ref[:, t * LANES : (t + 1) * LANES] for t in range(tiles)]
            peak = tree(jnp.maximum, q)
            peak_ref[rows, :] = peak
            total_ref[rows, :] = tree(jnp.add, [jnp.exp2(v - peak) for v in q])
        return carry

    lax.fori_loop(0, m // 16, step, 0)
    for a in range(m // LANES):
        rows = slice(a * LANES, (a + 1) * LANES)
        block = points_ref[rows, :]
        square = block * block
        folded = tree(jnp.add, [square[:, k : k + LANES] for k in range(0, block.shape[1], LANES)])
        norm_ref[a : a + 1, :] = lane_row(folded) * scale
        peak = peak_ref[rows, :].T
        total = total_ref[rows, :].T
        top = jnp.max(peak, axis=0, keepdims=True)
        value = top + jnp.log2(jnp.sum(total * jnp.exp2(peak - top), axis=0, keepdims=True))
        for d in range(out_ref.shape[0]):
            out_ref[d, a : a + 1, :] = value


def first_row_kernel(points_ref, high_ref, low_ref, shift_ref, scores_ref, norm_ref, out_ref, cols_ref, peak_ref, total_ref, *, scale):
    first_row_body(points_ref, high_ref, low_ref, shift_ref, scores_ref, norm_ref, out_ref, cols_ref, peak_ref, total_ref, scale)


def next_row_kernel(core_ref, own_ref, other_ref, high_ref, low_ref, shift_ref, scores_ref, norm_ref, out_ref, cols_ref, peak_ref, total_ref, points_ref, *, scale):
    join(core_ref, own_ref, other_ref, points_ref)
    first_row_body(points_ref, high_ref, low_ref, shift_ref, scores_ref, norm_ref, out_ref, cols_ref, peak_ref, total_ref, scale)


def join(core_ref, own_ref, other_ref, points_ref):
    half = points_ref.shape[0] // 2
    core = core_ref[0]
    for d in range(own_ref.shape[0]):
        points_ref[pl.ds(pl.multiple_of(core * half + d * ROWS, ROWS), ROWS), :] = own_ref[d]
        points_ref[pl.ds(pl.multiple_of((1 - core) * half + d * ROWS, ROWS), ROWS), :] = other_ref[d]


def join_kernel(core_ref, own_ref, other_ref, points_ref):
    join(core_ref, own_ref, other_ref, points_ref)


def first_col_kernel(parts_ref, norm_ref, scores_ref, dual_ref, out_ref, rows_ref, *, log_support):
    m, n = scores_ref.shape
    norm = norm_ref[...]
    log_total = log_combine(parts_ref[...]) - norm
    dual_ref[...] = (log_support - log_total) - norm
    spread_rows(dual_ref, rows_ref)
    group = 4
    for t in range(0, n // LANES, group):
        cols = [slice((t + k) * LANES, (t + k + 1) * LANES) for k in range(group)]

        def top(b, peaks):
            peaks = list(peaks)
            for s in range(4):
                rows = pl.ds(pl.multiple_of(b * 32 + s * 8, 8), 8)
                f = rows_ref[rows, :]
                for k in range(group):
                    peaks[k] = jnp.maximum(peaks[k], scores_ref[rows, cols[k]] + f)
            return tuple(peaks)

        start = tuple(jnp.full((8, LANES), -jnp.inf, F32) for k in range(group))
        peaks = lax.fori_loop(0, m // 32, top, start)

        def add(b, totals):
            totals = list(totals)
            for s in range(4):
                rows = pl.ds(pl.multiple_of(b * 32 + s * 8, 8), 8)
                f = rows_ref[rows, :]
                for k in range(group):
                    totals[k] = totals[k] + jnp.exp2((scores_ref[rows, cols[k]] + f) - peaks[k])
            return tuple(totals)

        zero = tuple(jnp.zeros((8, LANES), F32) for k in range(group))
        totals = lax.fori_loop(0, m // 32, add, zero)
        for k in range(group):
            best = jnp.max(peaks[k], axis=0, keepdims=True)
            value = best + jnp.log2(jnp.sum(totals[k] * jnp.exp2(peaks[k] - best), axis=0, keepdims=True))
            for d in range(out_ref.shape[0]):
                out_ref[d, t + k : t + k + 1, :] = value


def next_row_sum_kernel(parts_ref, norm_ref, weight_ref, scores_ref, dual_ref, plan_ref, col_dual_ref, out_ref, shift_ref, cols_ref, rows_ref, total_ref):
    m, n = scores_ref.shape
    norm = norm_ref[...]
    col_dual = jnp.log2(weight_ref[...]) - (log_combine(parts_ref[...]) - norm)
    col_dual_ref[...] = col_dual
    shift_ref[...] = col_dual - norm
    spread_cols(shift_ref, cols_ref)
    spread_rows(dual_ref, rows_ref)

    def step(b, carry):
        for half in range(2):
            rows = pl.ds(pl.multiple_of(b * 16 + half * 8, 8), 8)
            f = rows_ref[rows, :]
            plan = []
            for t in range(n // LANES):
                cols = slice(t * LANES, (t + 1) * LANES)
                value = jnp.exp2((scores_ref[rows, cols] + f) + cols_ref[:, cols])
                plan_ref[rows, cols] = value
                plan.append(value)
            total_ref[rows, :] = tree(jnp.add, plan)
        return carry

    lax.fori_loop(0, m // 16, step, 0)
    for a in range(m // LANES):
        value = lane_row(total_ref[a * LANES : (a + 1) * LANES, :])
        for d in range(out_ref.shape[0]):
            out_ref[d, a : a + 1, :] = value


def next_col_sum_kernel(parts_ref, plan_ref, factor_ref, out_ref, rows_ref, *, share):
    m, n = plan_ref.shape
    factor_ref[...] = share / jnp.sum(parts_ref[...], axis=0)
    spread_rows(factor_ref, rows_ref)
    tiles = n // LANES

    def step(b, totals):
        totals = list(totals)
        for s in range(4):
            rows = pl.ds(pl.multiple_of(b * 32 + s * 8, 8), 8)
            u = rows_ref[rows, :]
            for t in range(tiles):
                totals[t] = totals[t] + plan_ref[rows, t * LANES : (t + 1) * LANES] * u
        return tuple(totals)

    totals = lax.fori_loop(0, m // 32, step, tuple(jnp.zeros((8, LANES), F32) for t in range(tiles)))
    for t in range(tiles):
        value = jnp.sum(totals[t], axis=0, keepdims=True)
        for d in range(out_ref.shape[0]):
            out_ref[d, t : t + 1, :] = value


def move_kernel(core_ref, parts_ref, weight_ref, col_dual_ref, norm_ref, factor_ref, plan_ref, high_ref, low_ref, keep_ref, send_ref, next_dual_ref, shift_ref, scale_ref, cols_ref, rows_ref, total_ref, acc_ref, left_ref, rest_ref):
    m, n = plan_ref.shape
    tiles = n // LANES
    scale_ref[...] = weight_ref[...] / jnp.sum(parts_ref[...], axis=0)
    next_dual = col_dual_ref[...] + jnp.log2(scale_ref[...])
    next_dual_ref[...] = next_dual
    shift_ref[...] = next_dual - norm_ref[...]
    spread_cols(scale_ref, cols_ref)
    spread_rows(factor_ref, rows_ref)

    def step(b, carry):
        rows = pl.ds(pl.multiple_of(b * 16, 16), 16)
        u = rows_ref[rows, :]
        plan = []
        for t in range(tiles):
            cols = slice(t * LANES, (t + 1) * LANES)
            v = cols_ref[:, cols]
            value = plan_ref[rows, cols] * u * jnp.concatenate([v, v], axis=0)
            high, low = split(value)
            left_ref[rows, cols] = high
            rest_ref[rows, cols] = low
            plan.append(value)
        total_ref[rows, :] = tree(jnp.add, plan)
        return carry

    lax.fori_loop(0, m // 16, step, 0)
    xh = high_ref[...]
    xl = low_ref[...]
    for a in range(0, m, 256):
        left = left_ref[a : a + 256, :]
        acc = jnp.dot(left, xh, preferred_element_type=F32)
        acc = acc + jnp.dot(left, xl, preferred_element_type=F32)
        acc = acc + jnp.dot(rest_ref[a : a + 256, :], xh, preferred_element_type=F32)
        acc_ref[a : a + 256, :] = acc
    half = m // 2
    core = core_ref[0]
    for a in range(m // LANES):
        scale_ref[a : a + 1, :] = lane_row(total_ref[a * LANES : (a + 1) * LANES, :])
    for part, out_ref in ((core, keep_ref), (1 - core, send_ref)):
        for d in range(out_ref.shape[0]):
            out_ref[d, :ROWS, :] = acc_ref[pl.ds(pl.multiple_of(part * half + d * ROWS, ROWS), ROWS), :]
            mass = scale_ref[pl.ds(part * (half // LANES) + d // 2, 1), :]
            out_ref[d, ROWS:, :LANES] = jnp.broadcast_to(mass, (8, LANES))
            out_ref[d, ROWS:, LANES:] = jnp.zeros((8, out_ref.shape[2] - LANES), F32)


def add_kernel(a_ref, b_ref, out_ref):
    out_ref[...] = a_ref[...] + b_ref[...]


def divide_kernel(place_ref, parts_ref, out_ref, mass_ref):
    parts = tree(jnp.add, [parts_ref[d] for d in range(parts_ref.shape[0])])
    mass_ref[...] = jnp.broadcast_to(parts[ROWS : ROWS + 1, :LANES], (LANES, LANES)).T
    mass = mass_ref[pl.ds(pl.multiple_of((place_ref[0] % 2) * ROWS, ROWS), ROWS), :]
    width = parts.shape[1]
    points = parts[:ROWS, :] / jnp.concatenate([mass] * (width // LANES), axis=1)
    for d in range(out_ref.shape[0]):
        out_ref[d] = points


def call(kernel, outs, scratch, name, smem=0, **params):
    vmem = pl.BlockSpec(memory_space=pltpu.VMEM)

    def run(*args):
        specs = [pl.BlockSpec(memory_space=pltpu.SMEM)] * smem + [vmem] * (len(args) - smem)
        return pl.pallas_call(
            (lambda *refs: kernel(*refs, **params)),
            out_shape=outs,
            in_specs=specs,
            out_specs=jax.tree.map(lambda o: vmem, outs),
            scratch_shapes=scratch,
            name=name,
            compiler_params=pltpu.CompilerParams(vmem_limit_bytes=48 * 1024 * 1024),
        )(*args)

    return run


def body(support_points, data_points, data_weight):
    m, dim = support_points.shape
    n = data_points.shape[0]
    dp = lax.axis_size("dp")
    supp = lax.axis_size("supp")
    epsilon = dim / 16.0
    scale = math.log2(math.e) / epsilon
    total = m * supp
    place = lax.axis_index("dp")
    core = (place % 2).astype(jnp.int32).reshape(1)
    chip = (place // 2).astype(jnp.int32).reshape(1)
    chips = dp // 2
    pairs = [(k, k ^ 1) for k in range(dp)]
    groups = [[2 * k + c for k in range(chips)] for c in range(2)]
    mr, nr = m // LANES, n // LANES
    sds = jax.ShapeDtypeStruct
    scores_t = sds((m, n), F32)
    row_t, col_t = sds((mr, LANES), F32), sds((nr, LANES), F32)
    row_parts_t, col_parts_t = sds((dp, mr, LANES), F32), sds((supp, nr, LANES), F32)
    wide_t = sds((chips, ROWS + 8, dim), F32)
    points_t = sds((chips, ROWS, dim), F32)
    row_s, col_s = pltpu.VMEM((m, LANES), F32), pltpu.VMEM((8, n), F32)

    def over_dp(parts):
        return lax.all_to_all(parts, "dp", 0, 0)

    def over_supp(parts):
        return lax.all_to_all(parts, "supp", 0, 0)

    weight = data_weight.reshape(nr, LANES)
    high, low, col_norm = call(prepare_kernel, (sds((n, dim), BF16), sds((n, dim), BF16), col_t), [], "prepare", scale=scale)(data_points)
    shift = -col_norm
    for update_step in range(OUTER):
        outs = (scores_t, row_t, row_parts_t)
        scratch = [col_s, row_s, row_s]
        if update_step == 0:
            scores, row_norm, parts = call(first_row_kernel, outs, scratch, "row0", scale=scale)(support_points, high, low, shift)
        else:
            scratch = scratch + [pltpu.VMEM((m, dim), F32)]
            scores, row_norm, parts = call(next_row_kernel, outs, scratch, "row1", smem=1, scale=scale)(core, own, other, high, low, shift)
        parts = over_dp(parts)
        row_dual, parts = call(first_col_kernel, (row_t, col_parts_t), [row_s], "col", log_support=-math.log2(total))(parts, row_norm, scores)
        parts = over_supp(parts)
        plan, col_dual, parts = call(next_row_sum_kernel, (scores_t, col_t, row_parts_t), [pltpu.VMEM((nr, LANES), F32), col_s, row_s, row_s], "plan")(parts, col_norm, weight, scores, row_dual)
        parts = over_dp(parts)
        factor, parts = call(next_col_sum_kernel, (row_t, col_parts_t), [row_s], "colsum", share=1.0 / total)(parts, plan)
        parts = over_supp(parts)
        scratch = [pltpu.VMEM((nr, LANES), F32), col_s, row_s, row_s, pltpu.VMEM((m, dim), F32), pltpu.VMEM((m, n), BF16), pltpu.VMEM((m, n), BF16)]
        keep, send, col_dual, shift = call(move_kernel, (wide_t, wide_t, col_t, col_t), scratch, "move", smem=1)(core, parts, weight, col_dual, col_norm, factor, plan, high, low)
        got = lax.ppermute(send, "dp", pairs)
        wide = call(add_kernel, wide_t, [], "add")(keep, got)
        wide = lax.all_to_all(wide, "dp", 0, 0, axis_index_groups=groups)
        own = call(divide_kernel, points_t, [pltpu.VMEM((LANES, LANES), F32)], "divide", smem=1)(chip, wide)
        own = lax.all_to_all(own, "dp", 0, 0, axis_index_groups=groups)
        other = lax.ppermute(own, "dp", pairs)
    return call(join_kernel, sds((m, dim), F32), [], "join", smem=1)(core, own, other)


def solution(mesh):
    return jax.shard_map(
        body,
        mesh=mesh,
        in_specs=(P("supp", None), P("dp", None), P("dp")),
        out_specs=P("supp", None),
        check_vma=False,
    )
```

time: 915 us -> 250 us (0.27)
  blocking collectives: 595 us -> 122 us
  waiting for transfers between devices: 173 us -> 26.2 us
  Pallas kernels: 0 us -> 83.8 us
  other arithmetic: 78.3 us -> 0.01 us
  matrix products: 45.9 us -> 0 us
  starting transfers between devices: 0.04 us -> 14.5 us
  between operations: 14 us -> 0.13 us
    psum x10 -> x0, blocking collectives: 317 us -> none  [the longest x4 121 us: column_logsum(): totals = lax.psum(jnp.sum(jnp.exp(scores - peak[None, :]), axis=0), 'supp')]
    pmax x8 -> x0, blocking collectives: 278 us -> none  [the longest x4 139 us: row_logsum(): peak = lax.pmax(jnp.max(scores, axis=1), 'dp')]
    psum x2 -> x0, waiting for transfers between devices: 173 us -> none  [body(): weighted, masses = lax.psum((weighted, masses), 'dp')]
    all_to_all x0 -> x10, blocking collectives: none -> 122 us  [the longest x3 43.7 us: over_supp(): return lax.all_to_all(parts, 'supp', 0, 0)]
    pallas_call x0 -> x16, Pallas kernels: none -> 83.8 us  [run(): pl.pallas_call(lambda *refs: kernel(*refs, **params), out_shape=outs, in_...]
    reduce_sum x13 -> x0, other arithmetic: 50 us -> none  [the longest x4 18 us: column_logsum(): totals = lax.psum(jnp.sum(jnp.exp(scores - peak[None, :]), axis=0), 'supp')]
    dot_general x4 -> x0, matrix products: 45.9 us -> none  [the longest x2 23.8 us: body(): lax.dot_general(points, data_points, (((1,), (1,)), ((), ())), precision=...]
    reduce_max x6 -> x0, other arithmetic: 25.8 us -> none  [the longest x4 17.3 us: column_logsum(): peak = lax.pmax(jnp.max(scores, axis=0), 'supp')]
  transfers between devices with their start and end apart: 2 -> 6, of which waited for: 2 -> 6; matrix products, arithmetic and copies ran while one was open for 1% -> 0% of each run, Pallas kernels for 0% -> 0%
where the time goes in v1:
time: 250 us; the launch traced here: 249 us
  blocking collectives  122 us (49%)
  Pallas kernels  83.8 us (34%)
  waiting for transfers between devices  26.2 us (10%)
  starting transfers between devices  14.5 us (6%)
  local copies, waits for them, and re-layouts  2.81 us (1%)
    pallas_call x16, Pallas kernels, run(): pl.pallas_call(lambda *refs: kernel(*refs, **params), out_shape=outs, in_...  83.8 us
    all_to_all x3, blocking collectives, over_supp(): return lax.all_to_all(parts, 'supp', 0, 0)  43.7 us
    all_to_all x4, blocking collectives, over_dp(): return lax.all_to_all(parts, 'dp', 0, 0)  41.7 us
    all_to_all x2, blocking collectives, body(): own = lax.all_to_all(own, 'dp', 0, 0, axis_index_groups=groups)  23.1 us
    all_to_all x1, blocking collectives, body(): wide = lax.all_to_all(wide, 'dp', 0, 0, axis_index_groups=groups)  13.2 us
    all_to_all x1, waiting for transfers between devices, body(): wide = lax.all_to_all(wide, 'dp', 0, 0, axis_index_groups=groups)  10.9 us
    all_to_all x1, waiting for transfers between devices, over_supp(): return lax.all_to_all(parts, 'supp', 0, 0)  8.96 us
  transfers between devices with their start and end apart: 6, of which 6 were waited for; matrix products, arithmetic and copies ran while one was open for 0% of the time, Pallas kernels for 0%

profile of v1, /device:TPU:1, one launch (start us, length us, event | category | flops | bytes accessed | tf_op | source)
XLA Modules:
  0.0 249.1 jit_solution(12370517447780387357)
XLA Ops:
  0.0 0.0 copy-start
  0.0 1.6 copy-done
  1.6 0.0 copy-start.2
  1.6 0.5 prepare.1
  2.1 0.0 copy-start.1
  2.1 1.2 copy-done.1
  3.3 9.2 %row0.1 = (f32[1024,2048]{1,0:T(8,128)}, f32[8,128]{1,0:T(8,128)S(1)}, f32[16,8,128]{2,1,0:T(8,128)S(1)}) custom-call(f32[1024,256]{1,0:T(8,128)S(1)} %copy-done.1, bf16[2048,256]{1,0:T(8,128)(2,1)S(1)} %get-tuple-element.33.refs_1_.refs_7_.refs_3_, bf16[2048,256]{1,0:T(8,128)(2,1)S(1)} %get-tuple-element.34.refs_2_.refs_8_.refs_4_, f32[16,128]{1,0:T(8,128)S(1)} %neg.3.refs_3_), custom_call_target="tpu_custom_call" | custom-call | tf_op jit(solution)/shard_map/row0/pallas_call | solution.py:278
  12.5 12.4 %all_to_all.60.refs_0_ = f32[16,8,128]{2,1,0:T(8,128)S(1)} all-to-all(f32[16,8,128]{2,1,0:T(8,128)S(1)} %get-tuple-element.36), channel_id=1, replica_groups=mesh['dp'=16,'supp'=16] {'dp'}, dimensions={0} | all-to-all | bytes 131072 | tf_op jit(solution)/shard_map/all_to_all | solution.py:315
  24.9 7.7 %col.2 = (f32[8,128]{1,0:T(8,128)S(1)}, f32[16,16,128]{2,1,0:T(8,128)S(1)}) custom-call(f32[16,8,128]{2,1,0:T(8,128)S(1)} %all_to_all.60.refs_0_, f32[8,128]{1,0:T(8,128)S(1)} %get-tuple-element.37.refs_1_, f32[1024,2048]{1,0:T(8,128)} %get-tuple-element.38.refs_2_.refs_3_), custom_call_target="tpu_custom_call" | custom-call | tf_op jit(solution)/shard_map/col/pallas_call | solution.py:278
  32.6 19.3 %all_to_all.61.refs_0_ = f32[16,16,128]{2,1,0:T(8,128)S(1)} all-to-all(f32[16,16,128]{2,1,0:T(8,128)S(1)} %get-tuple-element.39), channel_id=1, replica_groups=mesh['dp'=16,'supp'=16] {'supp'}, dimensions={0} | all-to-all | bytes 262144 | tf_op jit(solution)/shard_map/all_to_all | solution.py:318
  52.0 0.0 copy-done.2
  52.0 9.0 %plan.2 = (f32[1024,2048]{1,0:T(8,128)}, f32[16,128]{1,0:T(8,128)S(1)}, f32[16,8,128]{2,1,0:T(8,128)S(1)}) custom-call(f32[16,16,128]{2,1,0:T(8,128)S(1)} %all_to_all.61.refs_0_, f32[16,128]{1,0:T(8,128)S(1)} %get-tuple-element.35.refs_1_.refs_4_, f32[16,128]{1,0:T(8,128)S(1)} %bitcast.3, f32[1024,2048]{1,0:T(8,128)} %get-tuple-element.38.refs_2_.refs_3_, ...), custom_call_target="tpu_custom_call" | custom-call | tf_op jit(solution)/shard_map/plan/pallas_call | solution.py:278
  61.0 10.3 %all_to_all.62.refs_0_ = f32[16,8,128]{2,1,0:T(8,128)S(1)} all-to-all(f32[16,8,128]{2,1,0:T(8,128)S(1)} %get-tuple-element.41), channel_id=1, replica_groups=mesh['dp'=16,'supp'=16] {'dp'}, dimensions={0} | all-to-all | bytes 131072 | tf_op jit(solution)/shard_map/all_to_all | solution.py:315
  71.3 5.1 %colsum.2 = (f32[8,128]{1,0:T(8,128)S(1)}, f32[16,16,128]{2,1,0:T(8,128)}) custom-call(f32[16,8,128]{2,1,0:T(8,128)S(1)} %all_to_all.62.refs_0_, f32[1024,2048]{1,0:T(8,128)} %get-tuple-element.42.refs_1_.refs_6_), custom_call_target="tpu_custom_call" | custom-call | tf_op jit(solution)/shard_map/colsum/pallas_call | solution.py:278
  76.4 3.5 %all-to-all-start.3 = ((f32[16,16,128]{2,1,0:T(8,128)}), f32[16,16,128]{2,1,0:T(8,128)S(1)}, u32[]{:S(2)}, u32[]{:S(2)}) async-start(f32[16,16,128]{2,1,0:T(8,128)} %get-tuple-element.43), calls=%async_computation.3 | async-start | bytes 262144 | tf_op jit(solution)/shard_map/all_to_all | solution.py:318
  79.9 9.0 %all-to-all-done.3.refs_1_ = f32[16,16,128]{2,1,0:T(8,128)S(1)} async-done(((f32[16,16,128]{2,1,0:T(8,128)}), f32[16,16,128]{2,1,0:T(8,128)S(1)}, u32[]{:S(2)}, u32[]{:S(2)}) %all-to-all-start.3) | async-done | bytes 131104 | tf_op jit(solution)/shard_map/all_to_all | solution.py:318
  88.9 9.6 %move.2 = (f32[8,72,256]{2,1,0:T(8,128)S(1)}, f32[8,72,256]{2,1,0:T(8,128)S(1)}, f32[16,128]{1,0:T(8,128)}, f32[16,128]{1,0:T(8,128)S(1)}) custom-call(s32[1]{0:T(128)} %bitcast.refs_0_, f32[16,16,128]{2,1,0:T(8,128)S(1)} %all-to-all-done.3.refs_1_, f32[16,128]{1,0:T(8,128)S(1)} %bitcast.4, f32[16,128]{1,0:T(8,128)S(1)} %get-tuple-element.44.refs_3_, ...), custom_call_target="tpu_custom_call" | custom-call | tf_op jit(solution)/shard_map/move/pallas_call | solution.py:278
  98.5 1.7 collective-permute-start
  100.2 1.6 collective-permute-done.refs_1_
  101.9 0.9 add.8
  102.7 3.5 %all-to-all-start.4 = ((f32[8,72,256]{2,1,0:T(8,128)}), f32[8,72,256]{2,1,0:T(8,128)S(1)}, u32[]{:S(2)}, u32[]{:S(2)}) async-start(f32[8,72,256]{2,1,0:T(8,128)} %add.8), calls=%async_computation.4 | async-start | bytes 1179648 | tf_op jit(solution)/shard_map/all_to_all | solution.py:342
  106.3 10.9 %all-to-all-done.4.refs_1_ = f32[8,72,256]{2,1,0:T(8,128)S(1)} async-done(((f32[8,72,256]{2,1,0:T(8,128)}), f32[8,72,256]{2,1,0:T(8,128)S(1)}, u32[]{:S(2)}, u32[]{:S(2)}) %all-to-all-start.4) | async-done | bytes 589856 | tf_op jit(solution)/shard_map/all_to_all | solution.py:342
  117.2 0.1 divide.2
  117.3 11.6 %all_to_all.63.refs_1_ = f32[8,64,256]{2,1,0:T(8,128)S(1)} all-to-all(f32[8,64,256]{2,1,0:T(8,128)S(1)} %divide.2), channel_id=1, replica_groups={{0,32,64,96,128,160,192,224},{16,48,80,112,144,176,208,240},{1,33,65,97..., dimensions={0} | all-to-all | bytes 1048576 | tf_op jit(solution)/shard_map/all_to_all | solution.py:344
  128.9 1.9 collective-permute-start.1
  130.8 1.5 collective-permute-done.1.refs_2_
  132.3 9.2 %row1.1 = (f32[1024,2048]{1,0:T(8,128)}, f32[8,128]{1,0:T(8,128)S(1)}, f32[16,8,128]{2,1,0:T(8,128)S(1)}) custom-call(s32[1]{0:T(128)} %bitcast.refs_0_, f32[8,64,256]{2,1,0:T(8,128)S(1)} %all_to_all.63.refs_1_, f32[8,64,256]{2,1,0:T(8,128)S(1)} %collective-permute-done.1.refs_2_, bf16[2048,256]{1,0:T(8,128)(2,1)S(1)} %get-tuple-element.33.refs_1_.refs_7_.refs_3_, ...), custom_call_target="tpu_custom_call" | custom-call | tf_op jit(solution)/shard_map/row1/pallas_call | solution.py:278
  141.5 8.7 %all_to_all.64.refs_0_ = f32[16,8,128]{2,1,0:T(8,128)S(1)} all-to-all(f32[16,8,128]{2,1,0:T(8,128)S(1)} %get-tuple-element.49), channel_id=1, replica_groups=mesh['dp'=16,'supp'=16] {'dp'}, dimensions={0} | all-to-all | bytes 131072 | tf_op jit(solution)/shard_map/all_to_all | solution.py:315
  150.3 7.7 %col.3 = (f32[8,128]{1,0:T(8,128)S(1)}, f32[16,16,128]{2,1,0:T(8,128)S(1)}) custom-call(f32[16,8,128]{2,1,0:T(8,128)S(1)} %all_to_all.64.refs_0_, f32[8,128]{1,0:T(8,128)S(1)} %get-tuple-element.50.refs_1_, f32[1024,2048]{1,0:T(8,128)} %get-tuple-element.51.refs_2_.refs_3_), custom_call_target="tpu_custom_call" | custom-call | tf_op jit(solution)/shard_map/col/pallas_call | solution.py:278
  157.9 12.1 %all_to_all.65.refs_0_ = f32[16,16,128]{2,1,0:T(8,128)S(1)} all-to-all(f32[16,16,128]{2,1,0:T(8,128)S(1)} %get-tuple-element.52), channel_id=1, replica_groups=mesh['dp'=16,'supp'=16] {'supp'}, dimensions={0} | all-to-all | bytes 262144 | tf_op jit(solution)/shard_map/all_to_all | solution.py:318
  170.0 9.0 %plan.3 = (f32[1024,2048]{1,0:T(8,128)}, f32[16,128]{1,0:T(8,128)S(1)}, f32[16,8,128]{2,1,0:T(8,128)S(1)}) custom-call(f32[16,16,128]{2,1,0:T(8,128)S(1)} %all_to_all.65.refs_0_, f32[16,128]{1,0:T(8,128)S(1)} %get-tuple-element.35.refs_1_.refs_4_, f32[16,128]{1,0:T(8,128)S(1)} %bitcast.5, f32[1024,2048]{1,0:T(8,128)} %get-tuple-element.51.refs_2_.refs_3_, ...), custom_call_target="tpu_custom_call" | custom-call | tf_op jit(solution)/shard_map/plan/pallas_call | solution.py:278
  179.1 10.3 %all_to_all.66.refs_0_ = f32[16,8,128]{2,1,0:T(8,128)S(1)} all-to-all(f32[16,8,128]{2,1,0:T(8,128)S(1)} %get-tuple-element.54), channel_id=1, replica_groups=mesh['dp'=16,'supp'=16] {'dp'}, dimensions={0} | all-to-all | bytes 131072 | tf_op jit(solution)/shard_map/all_to_all | solution.py:315
  189.3 4.4 %colsum.3 = (f32[8,128]{1,0:T(8,128)S(1)}, f32[16,16,128]{2,1,0:T(8,128)S(1)}) custom-call(f32[16,8,128]{2,1,0:T(8,128)S(1)} %all_to_all.66.refs_0_, f32[1024,2048]{1,0:T(8,128)} %get-tuple-element.55.refs_1_.refs_6_), custom_call_target="tpu_custom_call" | custom-call | tf_op jit(solution)/shard_map/colsum/pallas_call | solution.py:278
  193.8 12.2 %all_to_all.67.refs_1_ = f32[16,16,128]{2,1,0:T(8,128)S(1)} all-to-all(f32[16,16,128]{2,1,0:T(8,128)S(1)} %get-tuple-element.56), channel_id=1, replica_groups=mesh['dp'=16,'supp'=16] {'supp'}, dimensions={0} | all-to-all | bytes 262144 | tf_op jit(solution)/shard_map/all_to_all | solution.py:318
  206.0 10.0 %move.3 = (f32[8,72,256]{2,1,0:T(8,128)S(1)}, f32[8,72,256]{2,1,0:T(8,128)S(1)}, f32[16,128]{1,0:T(8,128)}, f32[16,128]{1,0:T(8,128)}) custom-call(s32[1]{0:T(128)} %bitcast.refs_0_, f32[16,16,128]{2,1,0:T(8,128)S(1)} %all_to_all.67.refs_1_, f32[16,128]{1,0:T(8,128)S(1)} %bitcast.6, f32[16,128]{1,0:T(8,128)S(1)} %get-tuple-element.57.refs_3_, ...), custom_call_target="tpu_custom_call" | custom-call | tf_op jit(solution)/shard_map/move/pallas_call | solution.py:278
  216.0 2.0 collective-permute-start.2
  218.0 1.6 collective-permute-done.2.refs_1_
  219.6 0.1 add.9
  219.7 13.2 %all_to_all.68.refs_1_ = f32[8,72,256]{2,1,0:T(8,128)S(1)} all-to-all(f32[8,72,256]{2,1,0:T(8,128)S(1)} %add.9), channel_id=1, replica_groups={{0,32,64,96,128,160,192,224},{16,48,80,112,144,176,208,240},{1,33,65,97..., dimensions={0} | all-to-all | bytes 1179648 | tf_op jit(solution)/shard_map/all_to_all | solution.py:342
  232.9 0.1 divide.3
  233.0 11.5 %all_to_all.69.refs_1_ = f32[8,64,256]{2,1,0:T(8,128)S(1)} all-to-all(f32[8,64,256]{2,1,0:T(8,128)S(1)} %divide.3), channel_id=1, replica_groups={{0,32,64,96,128,160,192,224},{16,48,80,112,144,176,208,240},{1,33,65,97..., dimensions={0} | all-to-all | bytes 1048576 | tf_op jit(solution)/shard_map/all_to_all | solution.py:344
  244.5 1.9 collective-permute-start.3
  246.5 1.5 collective-permute-done.3.refs_2_
  248.0 1.0 join.1
  (1 shorter events, 0.0 us)
Async XLA Ops:
  0.0 1.6 copy-start
  1.6 50.4 %copy-start.2 = (f32[2048]{0:T(1024)S(1)}, f32[2048]{0:T(1024)}, u32[]{:S(2)}) copy-start(f32[2048]{0:T(1024)} %param.5) | copy-start | bytes 24580
  2.1 1.2 copy-start.1
  76.4 12.5 %all-to-all-start.3 = ((f32[16,16,128]{2,1,0:T(8,128)}), f32[16,16,128]{2,1,0:T(8,128)S(1)}, u32[]{:S(2)}, u32[]{:S(2)}) async-start(f32[16,16,128]{2,1,0:T(8,128)} %get-tuple-element.43), calls=%async_computation.3 | async-start | bytes 262144 | tf_op jit(solution)/shard_map/all_to_all | solution.py:318
  98.5 3.3 %collective-permute-start = (f32[8,72,256]{2,1,0:T(8,128)S(1)}, f32[8,72,256]{2,1,0:T(8,128)S(1)}, u32[]{:S(2)}, u32[]{:S(2)}) collective-permute-start(f32[8,72,256]{2,1,0:T(8,128)S(1)} %get-tuple-element.47), channel_id=1, source_target_pairs={{0,16},{16,0},{32,48},{48,32},{64,80},{80,64},{96,112},{112,96},{1... | collective-permute-start | bytes 1769480 | tf_op jit(solution)/shard_map/ppermute | solution.py:340
  102.7 14.4 %all-to-all-start.4 = ((f32[8,72,256]{2,1,0:T(8,128)}), f32[8,72,256]{2,1,0:T(8,128)S(1)}, u32[]{:S(2)}, u32[]{:S(2)}) async-start(f32[8,72,256]{2,1,0:T(8,128)} %add.8), calls=%async_computation.4 | async-start | bytes 1179648 | tf_op jit(solution)/shard_map/all_to_all | solution.py:342
  128.9 3.4 %collective-permute-start.1 = (f32[8,64,256]{2,1,0:T(8,128)S(1)}, f32[8,64,256]{2,1,0:T(8,128)S(1)}, u32[]{:S(2)}, u32[]{:S(2)}) collective-permute-start(f32[8,64,256]{2,1,0:T(8,128)S(1)} %all_to_all.63.refs_1_), channel_id=1, source_target_pairs={{0,16},{16,0},{32,48},{48,32},{64,80},{80,64},{96,112},{112,96},{1... | collective-permute-start | bytes 1572872 | tf_op jit(solution)/shard_map/ppermute | solution.py:345
  216.0 3.6 %collective-permute-start.2 = (f32[8,72,256]{2,1,0:T(8,128)S(1)}, f32[8,72,256]{2,1,0:T(8,128)S(1)}, u32[]{:S(2)}, u32[]{:S(2)}) collective-permute-start(f32[8,72,256]{2,1,0:T(8,128)S(1)} %get-tuple-element.60), channel_id=1, source_target_pairs={{0,16},{16,0},{32,48},{48,32},{64,80},{80,64},{96,112},{112,96},{1... | collective-permute-start | bytes 1769480 | tf_op jit(solution)/shard_map/ppermute | solution.py:340
  244.5 3.5 %collective-permute-start.3 = (f32[8,64,256]{2,1,0:T(8,128)S(1)}, f32[8,64,256]{2,1,0:T(8,128)S(1)}, u32[]{:S(2)}, u32[]{:S(2)}) collective-permute-start(f32[8,64,256]{2,1,0:T(8,128)S(1)} %all_to_all.69.refs_1_), channel_id=1, source_target_pairs={{0,16},{16,0},{32,48},{48,32},{64,80},{80,64},{96,112},{112,96},{1... | collective-permute-start | bytes 1572872 | tf_op jit(solution)/shard_map/ppermute | solution.py:345

commit v2 on v1

--- a/solution.py
+++ b/solution.py
@@ -282,7 +282,7 @@
             out_specs=jax.tree.map(lambda o: vmem, outs),
             scratch_shapes=scratch,
             name=name,
-            compiler_params=pltpu.CompilerParams(vmem_limit_bytes=48 * 1024 * 1024),
+            compiler_params=pltpu.CompilerParams(vmem_limit_bytes=24 * 1024 * 1024),
         )(*args)
 
     return run

time: 250 us -> 218 us (0.87)
  Pallas kernels: 83.8 us -> 44.9 us
  local copies, waits for them, and re-layouts: 2.81 us -> 9.45 us
    pallas_call x16, Pallas kernels: 83.8 us -> 44.9 us  [run(): pl.pallas_call(lambda *refs: kernel(*refs, **params), out_shape=outs, in_...]
    unnamed x6 -> x10, local copies, waits for them, and re-layouts: 2.81 us -> 9.45 us
where the time goes in v2:
time: 218 us; the launch traced here: 217 us
  blocking collectives  122 us (56%)
  Pallas kernels  44.9 us (21%)
  waiting for transfers between devices  26.2 us (12%)
  starting transfers between devices  14.5 us (7%)
  local copies, waits for them, and re-layouts  9.45 us (4%)
    pallas_call x16, Pallas kernels, run(): pl.pallas_call(lambda *refs: kernel(*refs, **params), out_shape=outs, in_...  44.9 us
    all_to_all x3, blocking collectives, over_supp(): return lax.all_to_all(parts, 'supp', 0, 0)  43.7 us
    all_to_all x4, blocking collectives, over_dp(): return lax.all_to_all(parts, 'dp', 0, 0)  41.7 us
    all_to_all x2, blocking collectives, body(): own = lax.all_to_all(own, 'dp', 0, 0, axis_index_groups=groups)  23.1 us
    all_to_all x1, blocking collectives, body(): wide = lax.all_to_all(wide, 'dp', 0, 0, axis_index_groups=groups)  13.2 us
    all_to_all x1, waiting for transfers between devices, body(): wide = lax.all_to_all(wide, 'dp', 0, 0, axis_index_groups=groups)  10.9 us
    unnamed x10, local copies, waits for them, and re-layouts  9.45 us
    all_to_all x1, waiting for transfers between devices, over_supp(): return lax.all_to_all(parts, 'supp', 0, 0)  8.96 us
  transfers between devices with their start and end apart: 6, of which 6 were waited for; matrix products, arithmetic and copies ran while one was open for 0% of the time, Pallas kernels for 0%

profile of v2, /device:TPU:1, one launch (start us, length us, event | category | flops | bytes accessed | tf_op | source)
XLA Modules:
  0.0 216.9 jit_solution(14204966127174166893)
XLA Ops:
  0.0 0.0 copy-start.2
  0.0 1.6 copy-done.2
  1.6 0.0 copy-start.4
  1.6 0.5 prepare.1
  2.1 0.0 copy-start.3
  2.1 1.2 copy-done.3
  3.3 6.4 %row0.1 = (f32[1024,2048]{1,0:T(8,128)S(1)}, f32[8,128]{1,0:T(8,128)S(1)}, f32[16,8,128]{2,1,0:T(8,128)S(1)}) custom-call(f32[1024,256]{1,0:T(8,128)S(1)} %copy-done.3, bf16[2048,256]{1,0:T(8,128)(2,1)S(1)} %get-tuple-element.33.refs_1_.refs_7_.refs_3_, bf16[2048,256]{1,0:T(8,128)(2,1)S(1)} %get-tuple-element.34.refs_2_.refs_8_.refs_4_, ...), custom_call_target="tpu_custom_call" | custom-call | tf_op jit(solution)/shard_map/row0/pallas_call | solution.py:278
  9.7 12.4 %all_to_all.60.refs_0_ = f32[16,8,128]{2,1,0:T(8,128)S(1)} all-to-all(f32[16,8,128]{2,1,0:T(8,128)S(1)} %get-tuple-element.36), channel_id=1, replica_groups=mesh['dp'=16,'supp'=16] {'dp'}, dimensions={0} | all-to-all | bytes 131072 | tf_op jit(solution)/shard_map/all_to_all | solution.py:315
  22.2 4.3 %col.2 = (f32[8,128]{1,0:T(8,128)S(1)}, f32[16,16,128]{2,1,0:T(8,128)S(1)}) custom-call(f32[16,8,128]{2,1,0:T(8,128)S(1)} %all_to_all.60.refs_0_, f32[8,128]{1,0:T(8,128)S(1)} %get-tuple-element.37.refs_1_, f32[1024,2048]{1,0:T(8,128)S(1)} %get-tuple-element.38.refs_2_.refs_3_), custom_call_target="tpu_custom_call" | custom-call | tf_op jit(solution)/shard_map/col/pallas_call | solution.py:278
  26.5 19.4 %all_to_all.61.refs_0_ = f32[16,16,128]{2,1,0:T(8,128)S(1)} all-to-all(f32[16,16,128]{2,1,0:T(8,128)S(1)} %get-tuple-element.39), channel_id=1, replica_groups=mesh['dp'=16,'supp'=16] {'supp'}, dimensions={0} | all-to-all | bytes 262144 | tf_op jit(solution)/shard_map/all_to_all | solution.py:318
  45.8 0.0 copy-done.4
  45.8 2.6 %plan.2 = (f32[1024,2048]{1,0:T(8,128)S(1)}, f32[16,128]{1,0:T(8,128)S(1)}, f32[16,8,128]{2,1,0:T(8,128)S(1)}) custom-call(f32[16,16,128]{2,1,0:T(8,128)S(1)} %all_to_all.61.refs_0_, f32[16,128]{1,0:T(8,128)S(1)} %get-tuple-element.35.refs_1_.refs_4_, f32[16,128]{1,0:T(8,128)S(1)} %bitcast.3, f32[1024,2048]{1,0:T(8,128)S(1)} %get-tuple-element.38.refs_2_.refs_3_, ...), custom_call_target="tpu_custom_call" | custom-call | tf_op jit(solution)/shard_map/plan/pallas_call | solution.py:278
  48.4 10.3 %all_to_all.62.refs_0_ = f32[16,8,128]{2,1,0:T(8,128)S(1)} all-to-all(f32[16,8,128]{2,1,0:T(8,128)S(1)} %get-tuple-element.41), channel_id=1, replica_groups=mesh['dp'=16,'supp'=16] {'dp'}, dimensions={0} | all-to-all | bytes 131072 | tf_op jit(solution)/shard_map/all_to_all | solution.py:315
  58.7 1.7 colsum.2
  60.4 0.0 copy-start
  60.4 3.3 %copy-done = f32[1024,2048]{1,0:T(8,128)} copy-done((f32[1024,2048]{1,0:T(8,128)}, f32[1024,2048]{1,0:T(8,128)S(1)}, u32[]{:S(2)}) %copy-start) | copy-done | bytes 8388632
  63.7 3.5 %all-to-all-start.3 = ((f32[16,16,128]{2,1,0:T(8,128)}), f32[16,16,128]{2,1,0:T(8,128)S(1)}, u32[]{:S(2)}, u32[]{:S(2)}) async-start(f32[16,16,128]{2,1,0:T(8,128)} %get-tuple-element.43), calls=%async_computation.3 | async-start | bytes 262144 | tf_op jit(solution)/shard_map/all_to_all | solution.py:318
  67.2 9.0 %all-to-all-done.3.refs_1_ = f32[16,16,128]{2,1,0:T(8,128)S(1)} async-done(((f32[16,16,128]{2,1,0:T(8,128)}), f32[16,16,128]{2,1,0:T(8,128)S(1)}, u32[]{:S(2)}, u32[]{:S(2)}) %all-to-all-start.3) | async-done | bytes 131104 | tf_op jit(solution)/shard_map/all_to_all | solution.py:318
  76.2 0.0 copy-start.1
  76.2 3.4 %copy-done.1 = f32[1024,2048]{1,0:T(8,128)S(1)} copy-done((f32[1024,2048]{1,0:T(8,128)S(1)}, f32[1024,2048]{1,0:T(8,128)}, u32[]{:S(2)}) %copy-start.1) | copy-done | bytes 8388632
  79.5 6.3 %move.2 = (f32[8,72,256]{2,1,0:T(8,128)S(1)}, f32[8,72,256]{2,1,0:T(8,128)S(1)}, f32[16,128]{1,0:T(8,128)}, f32[16,128]{1,0:T(8,128)S(1)}) custom-call(s32[1]{0:T(128)} %bitcast.refs_0_, f32[16,16,128]{2,1,0:T(8,128)S(1)} %all-to-all-done.3.refs_1_, f32[16,128]{1,0:T(8,128)S(1)} %bitcast.4, f32[16,128]{1,0:T(8,128)S(1)} %get-tuple-element.44.refs_3_, ...), custom_call_target="tpu_custom_call" | custom-call | tf_op jit(solution)/shard_map/move/pallas_call | solution.py:278
  85.8 1.7 collective-permute-start
  87.5 1.6 collective-permute-done.refs_1_
  89.1 0.9 add.8
  90.0 3.5 %all-to-all-start.4 = ((f32[8,72,256]{2,1,0:T(8,128)}), f32[8,72,256]{2,1,0:T(8,128)S(1)}, u32[]{:S(2)}, u32[]{:S(2)}) async-start(f32[8,72,256]{2,1,0:T(8,128)} %add.8), calls=%async_computation.4 | async-start | bytes 1179648 | tf_op jit(solution)/shard_map/all_to_all | solution.py:342
  93.6 10.9 %all-to-all-done.4.refs_1_ = f32[8,72,256]{2,1,0:T(8,128)S(1)} async-done(((f32[8,72,256]{2,1,0:T(8,128)}), f32[8,72,256]{2,1,0:T(8,128)S(1)}, u32[]{:S(2)}, u32[]{:S(2)}) %all-to-all-start.4) | async-done | bytes 589856 | tf_op jit(solution)/shard_map/all_to_all | solution.py:342
  104.5 0.1 divide.2
  104.6 11.6 %all_to_all.63.refs_1_ = f32[8,64,256]{2,1,0:T(8,128)S(1)} all-to-all(f32[8,64,256]{2,1,0:T(8,128)S(1)} %divide.2), channel_id=1, replica_groups={{0,32,64,96,128,160,192,224},{16,48,80,112,144,176,208,240},{1,33,65,97..., dimensions={0} | all-to-all | bytes 1048576 | tf_op jit(solution)/shard_map/all_to_all | solution.py:344
  116.2 1.9 collective-permute-start.1
  118.1 1.5 collective-permute-done.1.refs_2_
  119.6 6.5 %row1.1 = (f32[1024,2048]{1,0:T(8,128)S(1)}, f32[8,128]{1,0:T(8,128)S(1)}, f32[16,8,128]{2,1,0:T(8,128)S(1)}) custom-call(s32[1]{0:T(128)} %bitcast.refs_0_, f32[8,64,256]{2,1,0:T(8,128)S(1)} %all_to_all.63.refs_1_, f32[8,64,256]{2,1,0:T(8,128)S(1)} %collective-permute-done.1.refs_2_, bf16[2048,256]{1,0:T(8,128)(2,1)S(1)} %get-tuple-element.33.refs_1_.refs_7_.refs_3_, ...), custom_call_target="tpu_custom_call" | custom-call | tf_op jit(solution)/shard_map/row1/pallas_call | solution.py:278
  126.1 8.7 %all_to_all.64.refs_0_ = f32[16,8,128]{2,1,0:T(8,128)S(1)} all-to-all(f32[16,8,128]{2,1,0:T(8,128)S(1)} %get-tuple-element.49), channel_id=1, replica_groups=mesh['dp'=16,'supp'=16] {'dp'}, dimensions={0} | all-to-all | bytes 131072 | tf_op jit(solution)/shard_map/all_to_all | solution.py:315
  134.8 4.3 %col.3 = (f32[8,128]{1,0:T(8,128)S(1)}, f32[16,16,128]{2,1,0:T(8,128)S(1)}) custom-call(f32[16,8,128]{2,1,0:T(8,128)S(1)} %all_to_all.64.refs_0_, f32[8,128]{1,0:T(8,128)S(1)} %get-tuple-element.50.refs_1_, f32[1024,2048]{1,0:T(8,128)S(1)} %get-tuple-element.51.refs_2_.refs_3_), custom_call_target="tpu_custom_call" | custom-call | tf_op jit(solution)/shard_map/col/pallas_call | solution.py:278
  139.1 12.1 %all_to_all.65.refs_0_ = f32[16,16,128]{2,1,0:T(8,128)S(1)} all-to-all(f32[16,16,128]{2,1,0:T(8,128)S(1)} %get-tuple-element.52), channel_id=1, replica_groups=mesh['dp'=16,'supp'=16] {'supp'}, dimensions={0} | all-to-all | bytes 262144 | tf_op jit(solution)/shard_map/all_to_all | solution.py:318
  151.2 2.6 %plan.3 = (f32[1024,2048]{1,0:T(8,128)S(1)}, f32[16,128]{1,0:T(8,128)S(1)}, f32[16,8,128]{2,1,0:T(8,128)S(1)}) custom-call(f32[16,16,128]{2,1,0:T(8,128)S(1)} %all_to_all.65.refs_0_, f32[16,128]{1,0:T(8,128)S(1)} %get-tuple-element.35.refs_1_.refs_4_, f32[16,128]{1,0:T(8,128)S(1)} %bitcast.5, f32[1024,2048]{1,0:T(8,128)S(1)} %get-tuple-element.51.refs_2_.refs_3_, ...), custom_call_target="tpu_custom_call" | custom-call | tf_op jit(solution)/shard_map/plan/pallas_call | solution.py:278
  153.8 10.3 %all_to_all.66.refs_0_ = f32[16,8,128]{2,1,0:T(8,128)S(1)} all-to-all(f32[16,8,128]{2,1,0:T(8,128)S(1)} %get-tuple-element.54), channel_id=1, replica_groups=mesh['dp'=16,'supp'=16] {'dp'}, dimensions={0} | all-to-all | bytes 131072 | tf_op jit(solution)/shard_map/all_to_all | solution.py:315
  164.0 1.1 colsum.3
  165.1 12.2 %all_to_all.67.refs_1_ = f32[16,16,128]{2,1,0:T(8,128)S(1)} all-to-all(f32[16,16,128]{2,1,0:T(8,128)S(1)} %get-tuple-element.56), channel_id=1, replica_groups=mesh['dp'=16,'supp'=16] {'supp'}, dimensions={0} | all-to-all | bytes 262144 | tf_op jit(solution)/shard_map/all_to_all | solution.py:318
  177.3 6.6 %move.3 = (f32[8,72,256]{2,1,0:T(8,128)S(1)}, f32[8,72,256]{2,1,0:T(8,128)S(1)}, f32[16,128]{1,0:T(8,128)}, f32[16,128]{1,0:T(8,128)}) custom-call(s32[1]{0:T(128)} %bitcast.refs_0_, f32[16,16,128]{2,1,0:T(8,128)S(1)} %all_to_all.67.refs_1_, f32[16,128]{1,0:T(8,128)S(1)} %bitcast.6, f32[16,128]{1,0:T(8,128)S(1)} %get-tuple-element.57.refs_3_, ...), custom_call_target="tpu_custom_call" | custom-call | tf_op jit(solution)/shard_map/move/pallas_call | solution.py:278
  183.9 2.0 collective-permute-start.2
  185.9 1.6 collective-permute-done.2.refs_1_
  187.5 0.1 add.9
  187.6 13.2 %all_to_all.68.refs_1_ = f32[8,72,256]{2,1,0:T(8,128)S(1)} all-to-all(f32[8,72,256]{2,1,0:T(8,128)S(1)} %add.9), channel_id=1, replica_groups={{0,32,64,96,128,160,192,224},{16,48,80,112,144,176,208,240},{1,33,65,97..., dimensions={0} | all-to-all | bytes 1179648 | tf_op jit(solution)/shard_map/all_to_all | solution.py:342
  200.8 0.1 divide.3
  200.9 11.5 %all_to_all.69.refs_1_ = f32[8,64,256]{2,1,0:T(8,128)S(1)} all-to-all(f32[8,64,256]{2,1,0:T(8,128)S(1)} %divide.3), channel_id=1, replica_groups={{0,32,64,96,128,160,192,224},{16,48,80,112,144,176,208,240},{1,33,65,97..., dimensions={0} | all-to-all | bytes 1048576 | tf_op jit(solution)/shard_map/all_to_all | solution.py:344
  212.4 1.9 collective-permute-start.3
  214.4 1.5 collective-permute-done.3.refs_2_
  215.9 1.0 join.1
  (1 shorter events, 0.0 us)
Async XLA Ops:
  0.0 1.6 copy-start.2
  1.6 44.2 %copy-start.4 = (f32[2048]{0:T(1024)S(1)}, f32[2048]{0:T(1024)}, u32[]{:S(2)}) copy-start(f32[2048]{0:T(1024)} %param.5) | copy-start | bytes 24580
  2.1 1.2 copy-start.3
  60.4 3.3 %copy-start = (f32[1024,2048]{1,0:T(8,128)}, f32[1024,2048]{1,0:T(8,128)S(1)}, u32[]{:S(2)}) copy-start(f32[1024,2048]{1,0:T(8,128)S(1)} %get-tuple-element.42.refs_1_.refs_6_) | copy-start | bytes 25165828
  63.7 12.5 %all-to-all-start.3 = ((f32[16,16,128]{2,1,0:T(8,128)}), f32[16,16,128]{2,1,0:T(8,128)S(1)}, u32[]{:S(2)}, u32[]{:S(2)}) async-start(f32[16,16,128]{2,1,0:T(8,128)} %get-tuple-element.43), calls=%async_computation.3 | async-start | bytes 262144 | tf_op jit(solution)/shard_map/all_to_all | solution.py:318
  76.2 3.4 %copy-start.1 = (f32[1024,2048]{1,0:T(8,128)S(1)}, f32[1024,2048]{1,0:T(8,128)}, u32[]{:S(2)}) copy-start(f32[1024,2048]{1,0:T(8,128)} %copy-done) | copy-start | bytes 25165828
  85.8 3.3 %collective-permute-start = (f32[8,72,256]{2,1,0:T(8,128)S(1)}, f32[8,72,256]{2,1,0:T(8,128)S(1)}, u32[]{:S(2)}, u32[]{:S(2)}) collective-permute-start(f32[8,72,256]{2,1,0:T(8,128)S(1)} %get-tuple-element.47), channel_id=1, source_target_pairs={{0,16},{16,0},{32,48},{48,32},{64,80},{80,64},{96,112},{112,96},{1... | collective-permute-start | bytes 1769480 | tf_op jit(solution)/shard_map/ppermute | solution.py:340
  90.0 14.4 %all-to-all-start.4 = ((f32[8,72,256]{2,1,0:T(8,128)}), f32[8,72,256]{2,1,0:T(8,128)S(1)}, u32[]{:S(2)}, u32[]{:S(2)}) async-start(f32[8,72,256]{2,1,0:T(8,128)} %add.8), calls=%async_computation.4 | async-start | bytes 1179648 | tf_op jit(solution)/shard_map/all_to_all | solution.py:342
  116.2 3.4 %collective-permute-start.1 = (f32[8,64,256]{2,1,0:T(8,128)S(1)}, f32[8,64,256]{2,1,0:T(8,128)S(1)}, u32[]{:S(2)}, u32[]{:S(2)}) collective-permute-start(f32[8,64,256]{2,1,0:T(8,128)S(1)} %all_to_all.63.refs_1_), channel_id=1, source_target_pairs={{0,16},{16,0},{32,48},{48,32},{64,80},{80,64},{96,112},{112,96},{1... | collective-permute-start | bytes 1572872 | tf_op jit(solution)/shard_map/ppermute | solution.py:345
  183.9 3.6 %collective-permute-start.2 = (f32[8,72,256]{2,1,0:T(8,128)S(1)}, f32[8,72,256]{2,1,0:T(8,128)S(1)}, u32[]{:S(2)}, u32[]{:S(2)}) collective-permute-start(f32[8,72,256]{2,1,0:T(8,128)S(1)} %get-tuple-element.60), channel_id=1, source_target_pairs={{0,16},{16,0},{32,48},{48,32},{64,80},{80,64},{96,112},{112,96},{1... | collective-permute-start | bytes 1769480 | tf_op jit(solution)/shard_map/ppermute | solution.py:340
  212.4 3.5 %collective-permute-start.3 = (f32[8,64,256]{2,1,0:T(8,128)S(1)}, f32[8,64,256]{2,1,0:T(8,128)S(1)}, u32[]{:S(2)}, u32[]{:S(2)}) collective-permute-start(f32[8,64,256]{2,1,0:T(8,128)S(1)} %all_to_all.69.refs_1_), channel_id=1, source_target_pairs={{0,16},{16,0},{32,48},{48,32},{64,80},{80,64},{96,112},{112,96},{1... | collective-permute-start | bytes 1572872 | tf_op jit(solution)/shard_map/ppermute | solution.py:345

commit v3 on v0

v3 whole, which is shorter than its diff:
```python
import math

import jax
import jax.numpy as jnp
from jax import lax
from jax.experimental import pallas as pl
from jax.experimental.pallas import tpu as pltpu
from jax.sharding import PartitionSpec as P

ITERS = 2
OUTER = 2
LANES = 128
ROWS = 64

F32 = jnp.float32
BF16 = jnp.bfloat16


def split(value):
    high = value.astype(BF16)
    low = (value - high.astype(F32)).astype(BF16)
    return high, low


def lane_row(block):
    return jnp.sum(block.T, axis=0, keepdims=True)


def spread_rows(vec_ref, out_ref):
    for a in range(vec_ref.shape[0]):
        block = jnp.broadcast_to(vec_ref[a : a + 1, :], (LANES, LANES))
        out_ref[a * LANES : (a + 1) * LANES, :] = block.T


def spread_cols(vec_ref, out_ref):
    for a in range(vec_ref.shape[0]):
        out_ref[:, a * LANES : (a + 1) * LANES] = jnp.broadcast_to(vec_ref[a : a + 1, :], (8, LANES))


def log_combine(parts):
    peak = jnp.max(parts, axis=0)
    return peak + jnp.log2(jnp.sum(jnp.exp2(parts - peak[None]), axis=0))


def tree(op, values):
    values = list(values)
    while len(values) > 1:
        values = [op(values[k], values[k + 1]) if k + 1 < len(values) else values[k] for k in range(0, len(values), 2)]
    return values[0]


def fold(block):
    return tree(jnp.add, [block[:, k : k + LANES] for k in range(0, block.shape[1], LANES)])


def prepare(x_ref, wide_ref, norm_ref, scale):
    dim = x_ref.shape[1]
    for a in range(x_ref.shape[0] // LANES):
        rows = slice(a * LANES, (a + 1) * LANES)
        block = x_ref[rows, :]
        high, low = split(block)
        wide_ref[rows, :dim] = high
        wide_ref[rows, dim : 2 * dim] = high
        wide_ref[rows, 2 * dim :] = low
        norm_ref[a : a + 1, :] = lane_row(fold(block * block)) * scale


def row_step(points_ref, wide_ref, shift_ref, scores_ref, plan_ref, norm_ref, top_ref, out_ref, cols_ref, peak_ref, total_ref, scale):
    m, n = scores_ref.shape
    tiles = n // LANES
    spread_cols(shift_ref, cols_ref)
    high, low = split(points_ref[...] * (2.0 * scale))
    left = jnp.concatenate([high, low, high], axis=1)
    for k in range(0, n, 256):
        acc = lax.dot_general(left, wide_ref[k : k + 256, :], (((1,), (1,)), ((), ())), preferred_element_type=F32)
        acc = acc + cols_ref[0:1, k : k + 256]
        scores_ref[:, k : k + 256] = acc
        best = jnp.maximum(acc[:, :LANES], acc[:, LANES:])
        peak_ref[...] = best if k == 0 else jnp.maximum(peak_ref[...], best)
    for a in range(m // LANES):
        rows = slice(a * LANES, (a + 1) * LANES)
        top = jnp.max(peak_ref[rows, :].T, axis=0, keepdims=True)
        top_ref[a : a + 1, :] = top
        peak_ref[rows, :] = jnp.broadcast_to(top, (LANES, LANES)).T

    def step(b, carry):
        for half in range(4):
            rows = pl.ds(pl.multiple_of(b * 32 + half * 8, 8), 8)
            peak = peak_ref[rows, :]
            values = []
            for t in range(tiles):
                cols = slice(t * LANES, (t + 1) * LANES)
                value = jnp.exp2(scores_ref[rows, cols] - peak)
                plan_ref[rows, cols] = value
                values.append(value)
            total_ref[rows, :] = tree(jnp.add, values)
        return carry

    lax.fori_loop(0, m // 32, step, 0)
    for a in range(m // LANES):
        rows = slice(a * LANES, (a + 1) * LANES)
        block = points_ref[rows, :]
        norm_ref[a : a + 1, :] = lane_row(fold(block * block)) * scale
        value = top_ref[a : a + 1, :] + jnp.log2(lane_row(total_ref[rows, :]))
        for d in range(out_ref.shape[0]):
            out_ref[d, a : a + 1, :] = value


def start_kernel(points_ref, x_ref, scores_ref, plan_ref, norm_ref, top_ref, out_ref, wide_ref, col_norm_ref, shift_ref, cols_ref, peak_ref, total_ref, *, scale):
    prepare(x_ref, wide_ref, col_norm_ref, scale)
    shift_ref[...] = -col_norm_ref[...]
    row_step(points_ref, wide_ref, shift_ref, scores_ref, plan_ref, norm_ref, top_ref, out_ref, cols_ref, peak_ref, total_ref, scale)


def next_row_kernel(own_ref, other_ref, wide_ref, shift_ref, scores_ref, plan_ref, norm_ref, top_ref, out_ref, cols_ref, peak_ref, total_ref, points_ref, *, scale):
    join(own_ref, other_ref, points_ref)
    row_step(points_ref, wide_ref, shift_ref, scores_ref, plan_ref, norm_ref, top_ref, out_ref, cols_ref, peak_ref, total_ref, scale)


def core_index():
    return lax.axis_index("dp") % 2


def join(own_ref, other_ref, points_ref):
    half = points_ref.shape[0] // 2
    core = core_index()
    for d in range(own_ref.shape[0]):
        points_ref[pl.ds(pl.multiple_of(core * half + d * ROWS, ROWS), ROWS), :] = own_ref[d]
        points_ref[pl.ds(pl.multiple_of((1 - core) * half + d * ROWS, ROWS), ROWS), :] = other_ref[d]


def join_kernel(own_ref, other_ref, points_ref):
    join(own_ref, other_ref, points_ref)


def column_sums(plan_ref, rows_ref):
    m, n = plan_ref.shape
    tiles = n // LANES

    def step(b, totals):
        totals = list(totals)
        for s in range(4):
            rows = pl.ds(pl.multiple_of(b * 32 + s * 8, 8), 8)
            u = rows_ref[rows, :]
            for t in range(tiles):
                totals[t] = totals[t] + plan_ref[rows, t * LANES : (t + 1) * LANES] * u
        return tuple(totals)

    totals = lax.fori_loop(0, m // 32, step, tuple(jnp.zeros((8, LANES), F32) for t in range(tiles)))
    return [jnp.sum(total, axis=0, keepdims=True) for total in totals]


def first_col_kernel(parts_ref, norm_ref, top_ref, shift_ref, scores_ref, plan_ref, dual_ref, out_ref, rows_ref, factor_ref, *, log_support):
    m, n = scores_ref.shape
    norm = norm_ref[...]
    log_total = log_combine(parts_ref[...]) - norm
    dual = (log_support - log_total) - norm
    dual_ref[...] = dual
    factor_ref[...] = jnp.exp2(dual + top_ref[...])
    spread_rows(factor_ref, rows_ref)
    sums = column_sums(plan_ref, rows_ref)
    for t, value in enumerate(sums):
        value = jnp.log2(value) - shift_ref[t : t + 1, :]
        for d in range(out_ref.shape[0]):
            out_ref[d, t : t + 1, :] = value

    @pl.when(jnp.min(tree(jnp.minimum, sums)) < 2.0**-80)
    def _():
        spread_rows(dual_ref, rows_ref)
        for t in range(n // LANES):
            cols = slice(t * LANES, (t + 1) * LANES)

            def top(b, peak):
                rows = pl.ds(pl.multiple_of(b * 8, 8), 8)
                return jnp.maximum(peak, scores_ref[rows, cols] + rows_ref[rows, :])

            peak = lax.fori_loop(0, m // 8, top, jnp.full((8, LANES), -jnp.inf, F32), unroll=8)
            best = jnp.max(peak, axis=0, keepdims=True)

            def add(b, total):
                rows = pl.ds(pl.multiple_of(b * 8, 8), 8)
                return total + jnp.exp2((scores_ref[rows, cols] + rows_ref[rows, :]) - best)

            total = lax.fori_loop(0, m // 8, add, jnp.zeros((8, LANES), F32), unroll=8)
            value = best + jnp.log2(jnp.sum(total, axis=0, keepdims=True)) - shift_ref[t : t + 1, :]
            for d in range(out_ref.shape[0]):
                out_ref[d, t : t + 1, :] = value


def next_row_sum_kernel(parts_ref, norm_ref, weight_ref, shift_ref, scores_ref, dual_ref, plan_ref, col_dual_ref, out_ref, delta_ref, cols_ref, rows_ref, total_ref):
    m, n = scores_ref.shape
    norm = norm_ref[...]
    col_dual = jnp.log2(weight_ref[...]) - (log_combine(parts_ref[...]) - norm)
    col_dual_ref[...] = col_dual
    delta_ref[...] = (col_dual - norm) - shift_ref[...]
    spread_cols(delta_ref, cols_ref)
    spread_rows(dual_ref, rows_ref)

    def step(b, carry):
        for half in range(4):
            rows = pl.ds(pl.multiple_of(b * 32 + half * 8, 8), 8)
            f = rows_ref[rows, :]
            plan = []
            for t in range(n // LANES):
                cols = slice(t * LANES, (t + 1) * LANES)
                value = jnp.exp2((scores_ref[rows, cols] + f) + cols_ref[:, cols])
                plan_ref[rows, cols] = value
                plan.append(value)
            total_ref[rows, :] = tree(jnp.add, plan)
        return carry

    lax.fori_loop(0, m // 32, step, 0)
    for a in range(m // LANES):
        value = lane_row(total_ref[a * LANES : (a + 1) * LANES, :])
        for d in range(out_ref.shape[0]):
            out_ref[d, a : a + 1, :] = value


def next_col_sum_kernel(parts_ref, plan_ref, factor_ref, out_ref, rows_ref, *, share):
    factor_ref[...] = share / jnp.sum(parts_ref[...], axis=0)
    spread_rows(factor_ref, rows_ref)
    for t, value in enumerate(column_sums(plan_ref, rows_ref)):
        for d in range(out_ref.shape[0]):
            out_ref[d, t : t + 1, :] = value


def move_half(half, plan_ref, factor_ref, ratio_ref, high_ref, low_ref, out_ref, rows_ref, mass_ref, acc_ref):
    n = plan_ref.shape[1]
    rows_here = plan_ref.shape[0] // 2
    spread_rows(factor_ref, rows_ref)
    high = high_ref[...]
    low = low_ref[...]
    for b in range(rows_here // 256):
        at = pl.ds(pl.multiple_of(half * rows_here + b * 256, 256), 256)
        plan = plan_ref[at, :]
        left, rest = split(plan)
        acc = jnp.dot(left, high, preferred_element_type=F32)
        acc = acc + jnp.dot(left, low, preferred_element_type=F32)
        acc = acc + jnp.dot(rest, high, preferred_element_type=F32)
        u = rows_ref[at, :]
        acc_ref[b * 256 : (b + 1) * 256, :] = acc * jnp.concatenate([u] * (acc.shape[1] // LANES), axis=1)
        mass = tree(jnp.add, [plan[:, t * LANES : (t + 1) * LANES] * ratio_ref[t : t + 1, :] for t in range(n // LANES)])
        mass = mass * u
        for a in range(2):
            mass_ref[2 * b + a : 2 * b + a + 1, :] = lane_row(mass[a * LANES : (a + 1) * LANES, :])
    for d in range(out_ref.shape[0]):
        points = acc_ref[d * ROWS : (d + 1) * ROWS, :]
        mass = jnp.broadcast_to(mass_ref[d // 2 : d // 2 + 1, :], (8, LANES))
        out_ref[d, :ROWS, :] = points
        out_ref[d, ROWS:, :LANES] = mass
        out_ref[d, ROWS:, LANES:] = jnp.zeros((8, out_ref.shape[2] - LANES), F32)


def send_kernel(parts_ref, weight_ref, col_dual_ref, norm_ref, factor_ref, plan_ref, x_ref, send_ref, high_ref, low_ref, ratio_ref, shift_ref, rows_ref, mass_ref, acc_ref):
    ratio_ref[...] = weight_ref[...] / jnp.sum(parts_ref[...], axis=0)
    shift_ref[...] = (col_dual_ref[...] + jnp.log2(ratio_ref[...])) - norm_ref[...]
    for a in range(x_ref.shape[0] // LANES):
        rows = slice(a * LANES, (a + 1) * LANES)
        v = jnp.broadcast_to(ratio_ref[a : a + 1, :], (LANES, LANES)).T
        high, low = split(x_ref[rows, :] * jnp.concatenate([v] * (x_ref.shape[1] // LANES), axis=1))
        high_ref[rows, :] = high
        low_ref[rows, :] = low
    move_half(1 - core_index(), plan_ref, factor_ref, ratio_ref, high_ref, low_ref, send_ref, rows_ref, mass_ref, acc_ref)


def keep_kernel(ratio_ref, factor_ref, plan_ref, high_ref, low_ref, out_ref, rows_ref, mass_ref, acc_ref):
    move_half(core_index(), plan_ref, factor_ref, ratio_ref, high_ref, low_ref, out_ref, rows_ref, mass_ref, acc_ref)


def add_kernel(a_ref, b_ref, out_ref):
    out_ref[...] = a_ref[...] + b_ref[...]


def divide_kernel(parts_ref, out_ref, mass_ref):
    parts = tree(jnp.add, [parts_ref[d] for d in range(parts_ref.shape[0])])
    mass_ref[...] = jnp.broadcast_to(parts[ROWS : ROWS + 1, :LANES], (LANES, LANES)).T
    mass = mass_ref[pl.ds(pl.multiple_of((lax.axis_index("dp") // 2 % 2) * ROWS, ROWS), ROWS), :]
    width = parts.shape[1]
    points = parts[:ROWS, :] / jnp.concatenate([mass] * (width // LANES), axis=1)
    for d in range(out_ref.shape[0]):
        out_ref[d] = points


def call(kernel, outs, scratch, name, **params):
    vmem = pl.BlockSpec(memory_space=pltpu.VMEM)

    def run(*args):
        return pl.pallas_call(
            (lambda *refs: kernel(*refs, **params)),
            out_shape=outs,
            in_specs=[vmem] * len(args),
            out_specs=jax.tree.map(lambda o: vmem, outs),
            scratch_shapes=scratch,
            name=name,
            compiler_params=pltpu.CompilerParams(vmem_limit_bytes=20 * 1024 * 1024),
        )(*args)

    return run


def body(support_points, data_points, data_weight):
    m, dim = support_points.shape
    n = data_points.shape[0]
    dp = lax.axis_size("dp")
    supp = lax.axis_size("supp")
    epsilon = dim / 16.0
    scale = math.log2(math.e) / epsilon
    total = m * supp
    chips = dp // 2
    pairs = [(k, k ^ 1) for k in range(dp)]
    groups = [[2 * k + c for k in range(chips)] for c in range(2)]
    mr, nr = m // LANES, n // LANES
    sds = jax.ShapeDtypeStruct
    scores_t = sds((m, n), F32)
    row_t, col_t = sds((mr, LANES), F32), sds((nr, LANES), F32)
    row_parts_t, col_parts_t = sds((dp, mr, LANES), F32), sds((supp, nr, LANES), F32)
    wide_t = sds((chips, ROWS + 8, dim), F32)
    points_t = sds((chips, ROWS, dim), F32)
    row_s, col_s = pltpu.VMEM((m, LANES), F32), pltpu.VMEM((8, n), F32)

    def over_dp(parts):
        return lax.all_to_all(parts, "dp", 0, 0)

    def over_supp(parts):
        return lax.all_to_all(parts, "supp", 0, 0)

    weight = data_weight.reshape(nr, LANES)
    half_t = sds((n, dim), BF16)
    mass_s = pltpu.VMEM((8, LANES), F32)
    acc_s = pltpu.VMEM((m // 2, dim), F32)
    for update_step in range(OUTER):
        outs = (scores_t, scores_t, row_t, row_t, row_parts_t)
        scratch = [col_s, row_s, row_s]
        if update_step == 0:
            outs = outs + (sds((n, 3 * dim), BF16), col_t, col_t)
            scores, raw, row_norm, top, parts, wide_x, col_norm, shift = call(start_kernel, outs, scratch, "row0", scale=scale)(support_points, data_points)
        else:
            scratch = scratch + [pltpu.VMEM((m, dim), F32)]
            scores, raw, row_norm, top, parts = call(next_row_kernel, outs, scratch, "row1", scale=scale)(own, other, wide_x, shift)
        parts = over_dp(parts)
        row_dual, parts = call(first_col_kernel, (row_t, col_parts_t), [row_s, pltpu.VMEM((mr, LANES), F32)], "col", log_support=-math.log2(total))(parts, row_norm, top, shift, scores, raw)
        parts = over_supp(parts)
        plan, col_dual, parts = call(next_row_sum_kernel, (scores_t, col_t, row_parts_t), [pltpu.VMEM((nr, LANES), F32), col_s, row_s, row_s], "plan")(parts, col_norm, weight, shift, scores, row_dual)
        parts = over_dp(parts)
        factor, parts = call(next_col_sum_kernel, (row_t, col_parts_t), [row_s], "colsum", share=1.0 / total)(parts, plan)
        parts = over_supp(parts)
        send, high, low, ratio, shift = call(send_kernel, (wide_t, half_t, half_t, col_t, col_t), [row_s, mass_s, acc_s], "send")(parts, weight, col_dual, col_norm, factor, plan, data_points)
        got = lax.ppermute(send, "dp", pairs)
        wide = call(keep_kernel, wide_t, [row_s, mass_s, acc_s], "keep")(ratio, factor, plan, high, low)
        wide = call(add_kernel, wide_t, [], "add")(wide, got)
        wide = lax.all_to_all(wide, "dp", 0, 0, axis_index_groups=groups)
        own = call(divide_kernel, points_t, [pltpu.VMEM((LANES, LANES), F32)], "divide")(wide)
        own = lax.all_to_all(own, "dp", 0, 0, axis_index_groups=groups)
        other = lax.ppermute(own, "dp", pairs)
    return call(join_kernel, sds((m, dim), F32), [], "join")(own, other)


def solution(mesh):
    return jax.shard_map(
        body,
        mesh=mesh,
        in_specs=(P("supp", None), P("dp", None), P("dp")),
        out_specs=P("supp", None),
        check_vma=False,
    )
```

time: 915 us -> 211 us (0.23)
  blocking collectives: 595 us -> 146 us
  waiting for transfers between devices: 173 us -> 3.08 us
  other arithmetic: 78.3 us -> 0 us
  Pallas kernels: 0 us -> 50.3 us
  matrix products: 45.9 us -> 0 us
  between operations: 14 us -> 0.13 us
    psum x10 -> x0, blocking collectives: 317 us -> none  [the longest x4 121 us: column_logsum(): totals = lax.psum(jnp.sum(jnp.exp(scores - peak[None, :]), axis=0), 'supp')]
    pmax x8 -> x0, blocking collectives: 278 us -> none  [the longest x4 139 us: row_logsum(): peak = lax.pmax(jnp.max(scores, axis=1), 'dp')]
    psum x2 -> x0, waiting for transfers between devices: 173 us -> none  [body(): weighted, masses = lax.psum((weighted, masses), 'dp')]
    all_to_all x0 -> x12, blocking collectives: none -> 146 us  [the longest x4 55.2 us: over_supp(): return lax.all_to_all(parts, 'supp', 0, 0)]
    pallas_call x0 -> x17, Pallas kernels: none -> 50.3 us  [run(): pl.pallas_call(lambda *refs: kernel(*refs, **params), out_shape=outs, in_...]
    reduce_sum x13 -> x0, other arithmetic: 50 us -> none  [the longest x4 18 us: column_logsum(): totals = lax.psum(jnp.sum(jnp.exp(scores - peak[None, :]), axis=0), 'supp')]
    dot_general x4 -> x0, matrix products: 45.9 us -> none  [the longest x2 23.8 us: body(): lax.dot_general(points, data_points, (((1,), (1,)), ((), ())), precision=...]
    reduce_max x6 -> x0, other arithmetic: 25.8 us -> none  [the longest x4 17.3 us: column_logsum(): peak = lax.pmax(jnp.max(scores, axis=0), 'supp')]
  transfers between devices with their start and end apart: 2 -> 4, of which waited for: 2 -> 2; matrix products, arithmetic and copies ran while one was open for 1% -> 0% of each run, Pallas kernels for 0% -> 2%
where the time goes in v3:
time: 211 us
  blocking collectives  146 us (69%)
  Pallas kernels  50.3 us (24%)
  starting transfers between devices  8.04 us (4%)
  waiting for transfers between devices  3.08 us (1%)
  local copies, waits for them, and re-layouts  2.82 us (1%)
    all_to_all x4, blocking collectives, over_supp(): return lax.all_to_all(parts, 'supp', 0, 0)  55.2 us
    pallas_call x17, Pallas kernels, run(): pl.pallas_call(lambda *refs: kernel(*refs, **params), out_shape=outs, in_...  50.3 us
    all_to_all x4, blocking collectives, over_dp(): return lax.all_to_all(parts, 'dp', 0, 0)  41.7 us
    all_to_all x2, blocking collectives, body(): wide = lax.all_to_all(wide, 'dp', 0, 0, axis_index_groups=groups)  26.2 us
    all_to_all x2, blocking collectives, body(): own = lax.all_to_all(own, 'dp', 0, 0, axis_index_groups=groups)  22.9 us
  transfers between devices with their start and end apart: 4, of which 2 were waited for; matrix products, arithmetic and copies ran while one was open for 0% of the time, Pallas kernels for 2%

profile of v3, /device:TPU:1, one launch (start us, length us, event | category | flops | bytes accessed | tf_op | source)
XLA Modules:
  0.0 210.5 jit_solution(13670570618142558789)
XLA Ops:
  0.0 0.0 copy-start
  0.0 1.6 copy-done
  1.6 0.0 copy-start.2
  1.6 1.2 copy-done.2
  2.8 5.8 %row0.1 = (f32[1024,2048]{1,0:T(8,128)S(1)}, f32[1024,2048]{1,0:T(8,128)S(1)}, f32[8,128]{1,0:T(8,128)S(1)}, f32[8,128]{1,0:T(8,128)S(1)}, f32[16,8,128]{2,1,0:T...) custom-call(f32[1024,256]{1,0:T(8,128)S(1)} %copy-done.2, ...), custom_call_target="tpu_custom_call" | custom-call | tf_op jit(solution)/shard_map/row0/pallas_call | solution.py:288
  8.6 12.4 %all_to_all.60.refs_0_ = f32[16,8,128]{2,1,0:T(8,128)S(1)} all-to-all(f32[16,8,128]{2,1,0:T(8,128)S(1)} %get-tuple-element.41), channel_id=1, replica_groups=mesh['dp'=16,'supp'=16] {'dp'}, dimensions={0} | all-to-all | bytes 131072 | tf_op jit(solution)/shard_map/all_to_all | solution.py:322
  21.0 0.0 copy-start.3
  21.0 10.2 %col.2 = (f32[8,128]{1,0:T(8,128)S(1)}, f32[16,16,128]{2,1,0:T(8,128)S(1)}) custom-call(f32[16,8,128]{2,1,0:T(8,128)S(1)} %all_to_all.60.refs_0_, f32[8,128]{1,0:T(8,128)S(1)} %get-tuple-element.42.refs_1_, f32[8,128]{1,0:T(8,128)S(1)} %get-tuple-element.43.refs_2_, f32[16,128]{1,0:T(8,128)S(1)} %get-tuple-element.44.refs_3_, ...), custom_call_target="tpu_custom_call" | custom-call | tf_op jit(solution)/shard_map/col/pallas_call | solution.py:288
  31.2 19.4 %all_to_all.61.refs_0_ = f32[16,16,128]{2,1,0:T(8,128)S(1)} all-to-all(f32[16,16,128]{2,1,0:T(8,128)S(1)} %get-tuple-element.47), channel_id=1, replica_groups=mesh['dp'=16,'supp'=16] {'supp'}, dimensions={0} | all-to-all | bytes 262144 | tf_op jit(solution)/shard_map/all_to_all | solution.py:325
  50.6 0.0 copy-done.3
  50.6 0.0 copy-start.1
  50.6 2.2 %plan.2 = (f32[1024,2048]{1,0:T(8,128)S(1)}, f32[16,128]{1,0:T(8,128)S(1)}, f32[16,8,128]{2,1,0:T(8,128)S(1)}) custom-call(f32[16,16,128]{2,1,0:T(8,128)S(1)} %all_to_all.61.refs_0_, f32[16,128]{1,0:T(8,128)S(1)} %get-tuple-element.48.refs_1_.refs_3_, f32[16,128]{1,0:T(8,128)S(1)} %bitcast.1, f32[16,128]{1,0:T(8,128)S(1)} %get-tuple-element.44.refs_3_, ...), custom_call_target="tpu_custom_call" | custom-call | tf_op jit(solution)/shard_map/plan/pallas_call | solution.py:288
  52.9 10.3 %all_to_all.62.refs_0_ = f32[16,8,128]{2,1,0:T(8,128)S(1)} all-to-all(f32[16,8,128]{2,1,0:T(8,128)S(1)} %get-tuple-element.50), channel_id=1, replica_groups=mesh['dp'=16,'supp'=16] {'dp'}, dimensions={0} | all-to-all | bytes 131072 | tf_op jit(solution)/shard_map/all_to_all | solution.py:322
  63.1 1.1 colsum.2
  64.2 11.8 %all_to_all.63.refs_0_ = f32[16,16,128]{2,1,0:T(8,128)S(1)} all-to-all(f32[16,16,128]{2,1,0:T(8,128)S(1)} %get-tuple-element.52), channel_id=1, replica_groups=mesh['dp'=16,'supp'=16] {'supp'}, dimensions={0} | all-to-all | bytes 262144 | tf_op jit(solution)/shard_map/all_to_all | solution.py:325
  76.0 0.0 copy-done.1
  76.0 2.6 %send.2 = (f32[8,72,256]{2,1,0:T(8,128)S(1)}, bf16[2048,256]{1,0:T(8,128)(2,1)S(1)}, bf16[2048,256]{1,0:T(8,128)(2,1)S(1)}, f32[16,128]{1,0:T(8,128)S(1)}, f32[16,128]{1,0:T(8,128)S(1)}) custom-call(f32[16,16,128]{2,1,0:T(8,128)S(1)} %all_to_all.63.refs_0_, f32[16,128]{1,0:T(8,128)S(1)} %bitcast.2, f32[16,128]{1,0:T(8,128)S(1)} %get-tuple-element.53.refs_2_, ...), custom_call_target="tpu_custom_call" | custom-call | tf_op jit(solution)/shard_map/send/pallas_call | solution.py:288
  78.6 2.1 collective-permute-start
  80.6 2.4 %keep.2.refs_0_ = f32[8,72,256]{2,1,0:T(8,128)S(1)} custom-call(f32[16,128]{1,0:T(8,128)S(1)} %get-tuple-element.55.refs_0_, f32[8,128]{1,0:T(8,128)S(1)} %get-tuple-element.54.refs_4_.refs_1_, f32[1024,2048]{1,0:T(8,128)S(1)} %get-tuple-element.51.refs_1_.refs_5_.refs_2_, bf16[2048,256]{1,0:T(8,128)(2,1)S(1)} %get-tuple-element.56.refs_3_, ...), custom_call_target="tpu_custom_call" | custom-call | tf_op jit(solution)/shard_map/keep/pallas_call | solution.py:288
  83.0 0.0 collective-permute-done.refs_1_
  83.0 0.1 add.2
  83.1 13.1 %all_to_all.64.refs_0_ = f32[8,72,256]{2,1,0:T(8,128)S(1)} all-to-all(f32[8,72,256]{2,1,0:T(8,128)S(1)} %add.2), channel_id=1, replica_groups={{0,32,64,96,128,160,192,224},{16,48,80,112,144,176,208,240},{1,33,65,97..., dimensions={0} | all-to-all | bytes 1179648 | tf_op jit(solution)/shard_map/all_to_all | solution.py:351
  96.2 0.1 divide.2
  96.4 11.5 %all_to_all.65.refs_0_ = f32[8,64,256]{2,1,0:T(8,128)S(1)} all-to-all(f32[8,64,256]{2,1,0:T(8,128)S(1)} %divide.2), channel_id=1, replica_groups={{0,32,64,96,128,160,192,224},{16,48,80,112,144,176,208,240},{1,33,65,97..., dimensions={0} | all-to-all | bytes 1048576 | tf_op jit(solution)/shard_map/all_to_all | solution.py:353
  107.9 2.0 collective-permute-start.1
  109.8 1.5 collective-permute-done.1.refs_1_
  111.4 5.8 %row1.1 = (f32[1024,2048]{1,0:T(8,128)S(1)}, f32[1024,2048]{1,0:T(8,128)S(1)}, f32[8,128]{1,0:T(8,128)S(1)}, f32[8,128]{1,0:T(8,128)S(1)}, f32[16,8,128]{2,1,0:T(8,128)S(1)}) custom-call(f32[8,64,256]{2,1,0:T(8,128)S(1)} %all_to_all.65.refs_0_, f32[8,64,256]{2,1,0:T(8,128)S(1)} %collective-permute-done.1.refs_1_, ...), custom_call_target="tpu_custom_call" | custom-call | tf_op jit(solution)/shard_map/row1/pallas_call | solution.py:288
  117.1 8.7 %all_to_all.66.refs_0_ = f32[16,8,128]{2,1,0:T(8,128)S(1)} all-to-all(f32[16,8,128]{2,1,0:T(8,128)S(1)} %get-tuple-element.61), channel_id=1, replica_groups=mesh['dp'=16,'supp'=16] {'dp'}, dimensions={0} | all-to-all | bytes 131072 | tf_op jit(solution)/shard_map/all_to_all | solution.py:322
  125.9 10.2 %col.3 = (f32[8,128]{1,0:T(8,128)S(1)}, f32[16,16,128]{2,1,0:T(8,128)S(1)}) custom-call(f32[16,8,128]{2,1,0:T(8,128)S(1)} %all_to_all.66.refs_0_, f32[8,128]{1,0:T(8,128)S(1)} %get-tuple-element.62.refs_1_, f32[8,128]{1,0:T(8,128)S(1)} %get-tuple-element.63.refs_2_, f32[16,128]{1,0:T(8,128)S(1)} %get-tuple-element.60.refs_3_, ...), custom_call_target="tpu_custom_call" | custom-call | tf_op jit(solution)/shard_map/col/pallas_call | solution.py:288
  136.1 12.1 %all_to_all.67.refs_0_ = f32[16,16,128]{2,1,0:T(8,128)S(1)} all-to-all(f32[16,16,128]{2,1,0:T(8,128)S(1)} %get-tuple-element.66), channel_id=1, replica_groups=mesh['dp'=16,'supp'=16] {'supp'}, dimensions={0} | all-to-all | bytes 262144 | tf_op jit(solution)/shard_map/all_to_all | solution.py:325
  148.2 2.2 %plan.3 = (f32[1024,2048]{1,0:T(8,128)S(1)}, f32[16,128]{1,0:T(8,128)S(1)}, f32[16,8,128]{2,1,0:T(8,128)S(1)}) custom-call(f32[16,16,128]{2,1,0:T(8,128)S(1)} %all_to_all.67.refs_0_, f32[16,128]{1,0:T(8,128)S(1)} %get-tuple-element.48.refs_1_.refs_3_, f32[16,128]{1,0:T(8,128)S(1)} %bitcast.3, f32[16,128]{1,0:T(8,128)S(1)} %get-tuple-element.60.refs_3_, ...), custom_call_target="tpu_custom_call" | custom-call | tf_op jit(solution)/shard_map/plan/pallas_call | solution.py:288
  150.4 10.3 %all_to_all.68.refs_0_ = f32[16,8,128]{2,1,0:T(8,128)S(1)} all-to-all(f32[16,8,128]{2,1,0:T(8,128)S(1)} %get-tuple-element.68), channel_id=1, replica_groups=mesh['dp'=16,'supp'=16] {'dp'}, dimensions={0} | all-to-all | bytes 131072 | tf_op jit(solution)/shard_map/all_to_all | solution.py:322
  160.7 1.1 colsum.3
  161.7 12.0 %all_to_all.69.refs_0_ = f32[16,16,128]{2,1,0:T(8,128)S(1)} all-to-all(f32[16,16,128]{2,1,0:T(8,128)S(1)} %get-tuple-element.70), channel_id=1, replica_groups=mesh['dp'=16,'supp'=16] {'supp'}, dimensions={0} | all-to-all | bytes 262144 | tf_op jit(solution)/shard_map/all_to_all | solution.py:325
  173.7 3.1 %send.3 = (f32[8,72,256]{2,1,0:T(8,128)S(1)}, bf16[2048,256]{1,0:T(8,128)(2,1)S(1)}, bf16[2048,256]{1,0:T(8,128)(2,1)S(1)}, f32[16,128]{1,0:T(8,128)S(1)}, f32[16,128]{1,0:T(8,128)}) custom-call(f32[16,16,128]{2,1,0:T(8,128)S(1)} %all_to_all.69.refs_0_, f32[16,128]{1,0:T(8,128)S(1)} %bitcast.4, f32[16,128]{1,0:T(8,128)S(1)} %get-tuple-element.71.refs_2_, ...), custom_call_target="tpu_custom_call" | custom-call | tf_op jit(solution)/shard_map/send/pallas_call | solution.py:288
  176.8 2.0 collective-permute-start.2
  178.8 2.4 %keep.3.refs_0_ = f32[8,72,256]{2,1,0:T(8,128)S(1)} custom-call(f32[16,128]{1,0:T(8,128)S(1)} %get-tuple-element.73.refs_0_, f32[8,128]{1,0:T(8,128)S(1)} %get-tuple-element.72.refs_4_.refs_1_, f32[1024,2048]{1,0:T(8,128)S(1)} %get-tuple-element.69.refs_1_.refs_5_.refs_2_, bf16[2048,256]{1,0:T(8,128)(2,1)S(1)} %get-tuple-element.74.refs_3_, ...), custom_call_target="tpu_custom_call" | custom-call | tf_op jit(solution)/shard_map/keep/pallas_call | solution.py:288
  181.1 0.0 collective-permute-done.2.refs_1_
  181.2 0.1 add.3
  181.2 13.1 %all_to_all.70.refs_0_ = f32[8,72,256]{2,1,0:T(8,128)S(1)} all-to-all(f32[8,72,256]{2,1,0:T(8,128)S(1)} %add.3), channel_id=1, replica_groups={{0,32,64,96,128,160,192,224},{16,48,80,112,144,176,208,240},{1,33,65,97..., dimensions={0} | all-to-all | bytes 1179648 | tf_op jit(solution)/shard_map/all_to_all | solution.py:351
  194.3 0.1 divide.3
  194.5 11.5 %all_to_all.71.refs_0_ = f32[8,64,256]{2,1,0:T(8,128)S(1)} all-to-all(f32[8,64,256]{2,1,0:T(8,128)S(1)} %divide.3), channel_id=1, replica_groups={{0,32,64,96,128,160,192,224},{16,48,80,112,144,176,208,240},{1,33,65,97..., dimensions={0} | all-to-all | bytes 1048576 | tf_op jit(solution)/shard_map/all_to_all | solution.py:353
  205.9 2.0 collective-permute-start.3
  207.9 1.5 collective-permute-done.3.refs_1_
  209.5 1.0 join.1
Async XLA Ops:
  0.0 1.6 copy-start
  1.6 1.2 copy-start.2
  21.0 29.6 %copy-start.3 = (f32[2048]{0:T(1024)S(1)}, f32[2048]{0:T(1024)}, u32[]{:S(2)}) copy-start(f32[2048]{0:T(1024)} %param.5) | copy-start | bytes 24580
  50.6 25.4 %copy-start.1 = (f32[2048,256]{1,0:T(8,128)S(1)}, f32[2048,256]{1,0:T(8,128)}, u32[]{:S(2)}) copy-start(f32[2048,256]{1,0:T(8,128)} %refs_6_.3) | copy-start | bytes 6291460
  78.6 4.4 %collective-permute-start = (f32[8,72,256]{2,1,0:T(8,128)S(1)}, f32[8,72,256]{2,1,0:T(8,128)S(1)}, u32[]{:S(2)}, u32[]{:S(2)}) collective-permute-start(f32[8,72,256]{2,1,0:T(8,128)S(1)} %get-tuple-element.58), channel_id=1, source_target_pairs={{0,16},{16,0},{32,48},{48,32},{64,80},{80,64},{96,112},{112,96},{1... | collective-permute-start | bytes 1769480 | tf_op jit(solution)/shard_map/ppermute | solution.py:348
  107.9 3.5 %collective-permute-start.1 = (f32[8,64,256]{2,1,0:T(8,128)S(1)}, f32[8,64,256]{2,1,0:T(8,128)S(1)}, u32[]{:S(2)}, u32[]{:S(2)}) collective-permute-start(f32[8,64,256]{2,1,0:T(8,128)S(1)} %all_to_all.65.refs_0_), channel_id=1, source_target_pairs={{0,16},{16,0},{32,48},{48,32},{64,80},{80,64},{96,112},{112,96},{1... | collective-permute-start | bytes 1572872 | tf_op jit(solution)/shard_map/ppermute | solution.py:354
  176.8 4.4 %collective-permute-start.2 = (f32[8,72,256]{2,1,0:T(8,128)S(1)}, f32[8,72,256]{2,1,0:T(8,128)S(1)}, u32[]{:S(2)}, u32[]{:S(2)}) collective-permute-start(f32[8,72,256]{2,1,0:T(8,128)S(1)} %get-tuple-element.76), channel_id=1, source_target_pairs={{0,16},{16,0},{32,48},{48,32},{64,80},{80,64},{96,112},{112,96},{1... | collective-permute-start | bytes 1769480 | tf_op jit(solution)/shard_map/ppermute | solution.py:348
  205.9 3.6 %collective-permute-start.3 = (f32[8,64,256]{2,1,0:T(8,128)S(1)}, f32[8,64,256]{2,1,0:T(8,128)S(1)}, u32[]{:S(2)}, u32[]{:S(2)}) collective-permute-start(f32[8,64,256]{2,1,0:T(8,128)S(1)} %all_to_all.71.refs_0_), channel_id=1, source_target_pairs={{0,16},{16,0},{32,48},{48,32},{64,80},{80,64},{96,112},{112,96},{1... | collective-permute-start | bytes 1572872 | tf_op jit(solution)/shard_map/ppermute | solution.py:354

commit v4 on v3

--- a/solution.py
+++ b/solution.py
@@ -53,9 +53,9 @@
     return tree(jnp.add, [block[:, k : k + LANES] for k in range(0, block.shape[1], LANES)])
 
 
-def prepare(x_ref, wide_ref, norm_ref, scale):
+def prepare(x_ref, wide_ref, norm_ref, scale, start, count):
     dim = x_ref.shape[1]
-    for a in range(x_ref.shape[0] // LANES):
+    for a in range(start // LANES, (start + count) // LANES):
         rows = slice(a * LANES, (a + 1) * LANES)
         block = x_ref[rows, :]
         high, low = split(block)
@@ -106,8 +106,17 @@
             out_ref[d, a : a + 1, :] = value
 
 
-def start_kernel(points_ref, x_ref, scores_ref, plan_ref, norm_ref, top_ref, out_ref, wide_ref, col_norm_ref, shift_ref, cols_ref, peak_ref, total_ref, *, scale):
-    prepare(x_ref, wide_ref, col_norm_ref, scale)
+def start_kernel(points_hbm, x_hbm, scores_ref, plan_ref, norm_ref, top_ref, out_ref, wide_ref, col_norm_ref, shift_ref, cols_ref, peak_ref, total_ref, points_ref, x_ref, sems, *, scale):
+    pieces = 4
+    count = x_ref.shape[0] // pieces
+    copies = [pltpu.make_async_copy(x_hbm.at[k * count : (k + 1) * count], x_ref.at[k * count : (k + 1) * count], sems.at[k]) for k in range(pieces)]
+    copies.append(pltpu.make_async_copy(points_hbm, points_ref, sems.at[pieces]))
+    for copy in copies:
+        copy.start()
+    for k in range(pieces):
+        copies[k].wait()
+        prepare(x_ref, wide_ref, col_norm_ref, scale, k * count, count)
+    copies[pieces].wait()
     shift_ref[...] = -col_norm_ref[...]
     row_step(points_ref, wide_ref, shift_ref, scores_ref, plan_ref, norm_ref, top_ref, out_ref, cols_ref, peak_ref, total_ref, scale)
 
@@ -129,8 +138,15 @@
         points_ref[pl.ds(pl.multiple_of((1 - core) * half + d * ROWS, ROWS), ROWS), :] = other_ref[d]
 
 
-def join_kernel(own_ref, other_ref, points_ref):
-    join(own_ref, other_ref, points_ref)
+def join_kernel(own_ref, other_ref, points_hbm, sems):
+    half = own_ref.shape[0]
+    core = core_index()
+    first = pltpu.make_async_copy(own_ref, points_hbm.at[pl.ds(pl.multiple_of(core * half, half), half)], sems.at[0])
+    second = pltpu.make_async_copy(other_ref, points_hbm.at[pl.ds(pl.multiple_of((1 - core) * half, half), half)], sems.at[1])
+    first.start()
+    second.start()
+    first.wait()
+    second.wait()
 
 
 def column_sums(plan_ref, rows_ref):
@@ -224,47 +240,44 @@
             out_ref[d, t : t + 1, :] = value
 
 
-def move_half(half, plan_ref, factor_ref, ratio_ref, high_ref, low_ref, out_ref, rows_ref, mass_ref, acc_ref):
+def move_half(half, plan_ref, factor_ref, ratio_ref, stack_ref, out_ref, rows_ref, mass_ref, acc_ref):
     n = plan_ref.shape[1]
     rows_here = plan_ref.shape[0] // 2
     spread_rows(factor_ref, rows_ref)
-    high = high_ref[...]
-    low = low_ref[...]
+    stack = stack_ref[...]
     for b in range(rows_here // 256):
         at = pl.ds(pl.multiple_of(half * rows_here + b * 256, 256), 256)
         plan = plan_ref[at, :]
         left, rest = split(plan)
-        acc = jnp.dot(left, high, preferred_element_type=F32)
-        acc = acc + jnp.dot(left, low, preferred_element_type=F32)
-        acc = acc + jnp.dot(rest, high, preferred_element_type=F32)
+        acc = jnp.dot(jnp.concatenate([left, left, rest], axis=1), stack, preferred_element_type=F32)
         u = rows_ref[at, :]
         acc_ref[b * 256 : (b + 1) * 256, :] = acc * jnp.concatenate([u] * (acc.shape[1] // LANES), axis=1)
         mass = tree(jnp.add, [plan[:, t * LANES : (t + 1) * LANES] * ratio_ref[t : t + 1, :] for t in range(n // LANES)])
         mass = mass * u
         for a in range(2):
             mass_ref[2 * b + a : 2 * b + a + 1, :] = lane_row(mass[a * LANES : (a + 1) * LANES, :])
+    tiles = acc_ref.shape[1] // LANES
     for d in range(out_ref.shape[0]):
-        points = acc_ref[d * ROWS : (d + 1) * ROWS, :]
-        mass = jnp.broadcast_to(mass_ref[d // 2 : d // 2 + 1, :], (8, LANES))
-        out_ref[d, :ROWS, :] = points
-        out_ref[d, ROWS:, :LANES] = mass
-        out_ref[d, ROWS:, LANES:] = jnp.zeros((8, out_ref.shape[2] - LANES), F32)
-
-
-def send_kernel(parts_ref, weight_ref, col_dual_ref, norm_ref, factor_ref, plan_ref, x_ref, send_ref, high_ref, low_ref, ratio_ref, shift_ref, rows_ref, mass_ref, acc_ref):
+        for t in range(tiles):
+            out_ref[d, t * ROWS : (t + 1) * ROWS, :] = acc_ref[d * ROWS : (d + 1) * ROWS, t * LANES : (t + 1) * LANES]
+        out_ref[d, tiles * ROWS :, :] = jnp.broadcast_to(mass_ref[d // 2 : d // 2 + 1, :], (8, LANES))
+
+
+def send_kernel(parts_ref, weight_ref, col_dual_ref, norm_ref, factor_ref, plan_ref, x_ref, send_ref, stack_ref, ratio_ref, shift_ref, rows_ref, mass_ref, acc_ref):
+    n = x_ref.shape[0]
     ratio_ref[...] = weight_ref[...] / jnp.sum(parts_ref[...], axis=0)
     shift_ref[...] = (col_dual_ref[...] + jnp.log2(ratio_ref[...])) - norm_ref[...]
-    for a in range(x_ref.shape[0] // LANES):
-        rows = slice(a * LANES, (a + 1) * LANES)
-        v = jnp.broadcast_to(ratio_ref[a : a + 1, :], (LANES, LANES)).T
-        high, low = split(x_ref[rows, :] * jnp.concatenate([v] * (x_ref.shape[1] // LANES), axis=1))
-        high_ref[rows, :] = high
-        low_ref[rows, :] = low
-    move_half(1 - core_index(), plan_ref, factor_ref, ratio_ref, high_ref, low_ref, send_ref, rows_ref, mass_ref, acc_ref)
-
-
-def keep_kernel(ratio_ref, factor_ref, plan_ref, high_ref, low_ref, out_ref, rows_ref, mass_ref, acc_ref):
-    move_half(core_index(), plan_ref, factor_ref, ratio_ref, high_ref, low_ref, out_ref, rows_ref, mass_ref, acc_ref)
+    for a in range(0, n, LANES):
+        v = jnp.broadcast_to(ratio_ref[a // LANES : a // LANES + 1, :], (LANES, LANES)).T
+        high, low = split(x_ref[a : a + LANES, :] * jnp.concatenate([v] * (x_ref.shape[1] // LANES), axis=1))
+        stack_ref[a : a + LANES, :] = high
+        stack_ref[n + a : n + a + LANES, :] = low
+        stack_ref[2 * n + a : 2 * n + a + LANES, :] = high
+    move_half(1 - core_index(), plan_ref, factor_ref, ratio_ref, stack_ref, send_ref, rows_ref, mass_ref, acc_ref)
+
+
+def keep_kernel(ratio_ref, factor_ref, plan_ref, stack_ref, out_ref, rows_ref, mass_ref, acc_ref):
+    move_half(core_index(), plan_ref, factor_ref, ratio_ref, stack_ref, out_ref, rows_ref, mass_ref, acc_ref)
 
 
 def add_kernel(a_ref, b_ref, out_ref):
@@ -273,23 +286,21 @@
 
 def divide_kernel(parts_ref, out_ref, mass_ref):
     parts = tree(jnp.add, [parts_ref[d] for d in range(parts_ref.shape[0])])
-    mass_ref[...] = jnp.broadcast_to(parts[ROWS : ROWS + 1, :LANES], (LANES, LANES)).T
+    tiles = out_ref.shape[2] // LANES
+    mass_ref[...] = jnp.broadcast_to(parts[tiles * ROWS : tiles * ROWS + 1, :], (LANES, LANES)).T
     mass = mass_ref[pl.ds(pl.multiple_of((lax.axis_index("dp") // 2 % 2) * ROWS, ROWS), ROWS), :]
-    width = parts.shape[1]
-    points = parts[:ROWS, :] / jnp.concatenate([mass] * (width // LANES), axis=1)
+    points = jnp.concatenate([parts[t * ROWS : (t + 1) * ROWS, :] / mass for t in range(tiles)], axis=1)
     for d in range(out_ref.shape[0]):
         out_ref[d] = points
 
 
-def call(kernel, outs, scratch, name, **params):
-    vmem = pl.BlockSpec(memory_space=pltpu.VMEM)
-
+def call(kernel, outs, scratch, name, inputs=pltpu.VMEM, outputs=pltpu.VMEM, **params):
     def run(*args):
         return pl.pallas_call(
             (lambda *refs: kernel(*refs, **params)),
             out_shape=outs,
-            in_specs=[vmem] * len(args),
-            out_specs=jax.tree.map(lambda o: vmem, outs),
+            in_specs=[pl.BlockSpec(memory_space=inputs)] * len(args),
+            out_specs=jax.tree.map(lambda o: pl.BlockSpec(memory_space=outputs), outs),
             scratch_shapes=scratch,
             name=name,
             compiler_params=pltpu.CompilerParams(vmem_limit_bytes=20 * 1024 * 1024),
@@ -314,7 +325,7 @@
     scores_t = sds((m, n), F32)
     row_t, col_t = sds((mr, LANES), F32), sds((nr, LANES), F32)
     row_parts_t, col_parts_t = sds((dp, mr, LANES), F32), sds((supp, nr, LANES), F32)
-    wide_t = sds((chips, ROWS + 8, dim), F32)
+    wide_t = sds((chips, ROWS * (dim // LANES) + 8, LANES), F32)
     points_t = sds((chips, ROWS, dim), F32)
     row_s, col_s = pltpu.VMEM((m, LANES), F32), pltpu.VMEM((8, n), F32)
 
@@ -325,7 +336,7 @@
         return lax.all_to_all(parts, "supp", 0, 0)
 
     weight = data_weight.reshape(nr, LANES)
-    half_t = sds((n, dim), BF16)
+    stack_t = sds((3 * n, dim), BF16)
     mass_s = pltpu.VMEM((8, LANES), F32)
     acc_s = pltpu.VMEM((m // 2, dim), F32)
     for update_step in range(OUTER):
@@ -333,7 +344,7 @@
         scratch = [col_s, row_s, row_s]
         if update_step == 0:
             outs = outs + (sds((n, 3 * dim), BF16), col_t, col_t)
-            scores, raw, row_norm, top, parts, wide_x, col_norm, shift = call(start_kernel, outs, scratch, "row0", scale=scale)(support_points, data_points)
+            scores, raw, row_norm, top, parts, wide_x, col_norm, shift = call(start_kernel, outs, scratch + [pltpu.VMEM((m, dim), F32), pltpu.VMEM((n, dim), F32), pltpu.SemaphoreType.DMA((5,))], "row0", inputs=pltpu.HBM, scale=scale)(*[pltpu.with_memory_space_constraint(v, pltpu.HBM) for v in (support_points, data_points)])
         else:
             scratch = scratch + [pltpu.VMEM((m, dim), F32)]
             scores, raw, row_norm, top, parts = call(next_row_kernel, outs, scratch, "row1", scale=scale)(own, other, wide_x, shift)
@@ -344,15 +355,16 @@
         parts = over_dp(parts)
         factor, parts = call(next_col_sum_kernel, (row_t, col_parts_t), [row_s], "colsum", share=1.0 / total)(parts, plan)
         parts = over_supp(parts)
-        send, high, low, ratio, shift = call(send_kernel, (wide_t, half_t, half_t, col_t, col_t), [row_s, mass_s, acc_s], "send")(parts, weight, col_dual, col_norm, factor, plan, data_points)
+        send, stack, ratio, shift = call(send_kernel, (wide_t, stack_t, col_t, col_t), [row_s, mass_s, acc_s], "send")(parts, weight, col_dual, col_norm, factor, plan, data_points)
         got = lax.ppermute(send, "dp", pairs)
-        wide = call(keep_kernel, wide_t, [row_s, mass_s, acc_s], "keep")(ratio, factor, plan, high, low)
+        wide = call(keep_kernel, wide_t, [row_s, mass_s, acc_s], "keep")(ratio, factor, plan, stack)
         wide = call(add_kernel, wide_t, [], "add")(wide, got)
         wide = lax.all_to_all(wide, "dp", 0, 0, axis_index_groups=groups)
         own = call(divide_kernel, points_t, [pltpu.VMEM((LANES, LANES), F32)], "divide")(wide)
         own = lax.all_to_all(own, "dp", 0, 0, axis_index_groups=groups)
         other = lax.ppermute(own, "dp", pairs)
-    return call(join_kernel, sds((m, dim), F32), [], "join")(own, other)
+    halves = (own.reshape(m // 2, dim), other.reshape(m // 2, dim))
+    return call(join_kernel, sds((m, dim), F32), [pltpu.SemaphoreType.DMA((2,))], "join", outputs=pltpu.HBM)(*halves)
 
 
 def solution(mesh):

time: 211 us -> 210 us (level)
  local copies, waits for them, and re-layouts: 2.82 us -> 0.01 us
    unnamed x8 -> x4, local copies, waits for them, and re-layouts: 2.82 us -> 0.01 us
where the time goes in v4:
time: 210 us; the launch traced here: 209 us
  blocking collectives  145 us (69%)
  Pallas kernels  52.1 us (25%)
  starting transfers between devices  8.1 us (4%)
  waiting for transfers between devices  3.08 us (1%)
    all_to_all x4, blocking collectives, over_supp(): return lax.all_to_all(parts, 'supp', 0, 0)  55.2 us
    pallas_call x17, Pallas kernels, run(): pl.pallas_call(lambda *refs: kernel(*refs, **params), out_shape=outs, in_...  52.1 us
    all_to_all x4, blocking collectives, over_dp(): return lax.all_to_all(parts, 'dp', 0, 0)  41.7 us
    all_to_all x2, blocking collectives, body(): wide = lax.all_to_all(wide, 'dp', 0, 0, axis_index_groups=groups)  25.6 us
    all_to_all x2, blocking collectives, body(): own = lax.all_to_all(own, 'dp', 0, 0, axis_index_groups=groups)  22.9 us
  transfers between devices with their start and end apart: 4, of which 2 were waited for; matrix products, arithmetic and copies ran while one was open for 0% of the time, Pallas kernels for 2%

profile of v4, /device:TPU:1, one launch (start us, length us, event | category | flops | bytes accessed | tf_op | source)
XLA Modules:
  0.0 209.0 jit_solution(9301293588671137439)
XLA Ops:
  0.0 7.6 %row0.1 = (f32[1024,2048]{1,0:T(8,128)S(1)}, f32[1024,2048]{1,0:T(8,128)S(1)}, f32[8,128]{1,0:T(8,128)S(1)}, f32[8,128]{1,0:T(8,128)S(1)}, f32[16,8,128]{2,1,0:T...) custom-call(f32[1024,256]{1,0:T(8,128)} %refs_0_.1, f32[2048,256]{1,0:T(8,128)} %refs_6_.3), custom_call_target="tpu_custom_call" | custom-call | tf_op jit(solution)/shard_map/row0/pallas_call | solution.py:299
  7.6 12.4 %all_to_all.60.refs_0_ = f32[16,8,128]{2,1,0:T(8,128)S(1)} all-to-all(f32[16,8,128]{2,1,0:T(8,128)S(1)} %get-tuple-element.39), channel_id=1, replica_groups=mesh['dp'=16,'supp'=16] {'dp'}, dimensions={0} | all-to-all | bytes 131072 | tf_op jit(solution)/shard_map/all_to_all | solution.py:333
  20.0 0.0 copy-start.1
  20.1 10.2 %col.2 = (f32[8,128]{1,0:T(8,128)S(1)}, f32[16,16,128]{2,1,0:T(8,128)S(1)}) custom-call(f32[16,8,128]{2,1,0:T(8,128)S(1)} %all_to_all.60.refs_0_, f32[8,128]{1,0:T(8,128)S(1)} %get-tuple-element.40.refs_1_, f32[8,128]{1,0:T(8,128)S(1)} %get-tuple-element.41.refs_2_, f32[16,128]{1,0:T(8,128)S(1)} %get-tuple-element.42.refs_3_, ...), custom_call_target="tpu_custom_call" | custom-call | tf_op jit(solution)/shard_map/col/pallas_call | solution.py:299
  30.2 19.4 %all_to_all.61.refs_0_ = f32[16,16,128]{2,1,0:T(8,128)S(1)} all-to-all(f32[16,16,128]{2,1,0:T(8,128)S(1)} %get-tuple-element.45), channel_id=1, replica_groups=mesh['dp'=16,'supp'=16] {'supp'}, dimensions={0} | all-to-all | bytes 262144 | tf_op jit(solution)/shard_map/all_to_all | solution.py:336
  49.6 0.0 copy-done.1
  49.6 0.0 copy-start
  49.6 2.2 %plan.2 = (f32[1024,2048]{1,0:T(8,128)S(1)}, f32[16,128]{1,0:T(8,128)S(1)}, f32[16,8,128]{2,1,0:T(8,128)S(1)}) custom-call(f32[16,16,128]{2,1,0:T(8,128)S(1)} %all_to_all.61.refs_0_, f32[16,128]{1,0:T(8,128)S(1)} %get-tuple-element.46.refs_1_.refs_3_, f32[16,128]{1,0:T(8,128)S(1)} %bitcast.5, f32[16,128]{1,0:T(8,128)S(1)} %get-tuple-element.42.refs_3_, ...), custom_call_target="tpu_custom_call" | custom-call | tf_op jit(solution)/shard_map/plan/pallas_call | solution.py:299
  51.9 10.3 %all_to_all.62.refs_0_ = f32[16,8,128]{2,1,0:T(8,128)S(1)} all-to-all(f32[16,8,128]{2,1,0:T(8,128)S(1)} %get-tuple-element.48), channel_id=1, replica_groups=mesh['dp'=16,'supp'=16] {'dp'}, dimensions={0} | all-to-all | bytes 131072 | tf_op jit(solution)/shard_map/all_to_all | solution.py:333
  62.1 1.1 colsum.2
  63.2 11.8 %all_to_all.63.refs_0_ = f32[16,16,128]{2,1,0:T(8,128)S(1)} all-to-all(f32[16,16,128]{2,1,0:T(8,128)S(1)} %get-tuple-element.50), channel_id=1, replica_groups=mesh['dp'=16,'supp'=16] {'supp'}, dimensions={0} | all-to-all | bytes 262144 | tf_op jit(solution)/shard_map/all_to_all | solution.py:336
  75.0 0.0 copy-done
  75.0 2.6 %send.2 = (f32[8,136,128]{2,1,0:T(8,128)S(1)}, bf16[6144,256]{1,0:T(8,128)(2,1)S(1)}, f32[16,128]{1,0:T(8,128)S(1)}, f32[16,128]{1,0:T(8,128)S(1)}) custom-call(f32[16,16,128]{2,1,0:T(8,128)S(1)} %all_to_all.63.refs_0_, f32[16,128]{1,0:T(8,128)S(1)} %bitcast.6, f32[16,128]{1,0:T(8,128)S(1)} %get-tuple-element.51.refs_2_, ...), custom_call_target="tpu_custom_call" | custom-call | tf_op jit(solution)/shard_map/send/pallas_call | solution.py:299
  77.6 2.1 collective-permute-start
  79.6 2.3 %keep.2.refs_0_ = f32[8,136,128]{2,1,0:T(8,128)S(1)} custom-call(f32[16,128]{1,0:T(8,128)S(1)} %get-tuple-element.53.refs_0_, f32[8,128]{1,0:T(8,128)S(1)} %get-tuple-element.52.refs_4_.refs_1_, f32[1024,2048]{1,0:T(8,128)S(1)} %get-tuple-element.49.refs_1_.refs_5_.refs_2_, bf16[6144,256]{1,0:T(8,128)(2,1)S(1)} %get-tuple-element.54.refs_3_), custom_call_target="tpu_custom_call" | custom-call | tf_op jit(solution)/shard_map/keep/pallas_call | solution.py:299
  82.0 0.0 collective-permute-done.refs_1_
  82.0 0.1 add.2
  82.1 12.8 %all_to_all.64.refs_0_ = f32[8,136,128]{2,1,0:T(8,128)S(1)} all-to-all(f32[8,136,128]{2,1,0:T(8,128)S(1)} %add.2), channel_id=1, replica_groups={{0,32,64,96,128,160,192,224},{16,48,80,112,144,176,208,240},{1,33,65,97..., dimensions={0} | all-to-all | bytes 1114112 | tf_op jit(solution)/shard_map/all_to_all | solution.py:362
  94.9 0.1 divide.2
  95.0 11.4 %all_to_all.65.refs_0_ = f32[8,64,256]{2,1,0:T(8,128)S(1)} all-to-all(f32[8,64,256]{2,1,0:T(8,128)S(1)} %divide.2), channel_id=1, replica_groups={{0,32,64,96,128,160,192,224},{16,48,80,112,144,176,208,240},{1,33,65,97..., dimensions={0} | all-to-all | bytes 1048576 | tf_op jit(solution)/shard_map/all_to_all | solution.py:364
  106.5 2.0 collective-permute-start.1
  108.5 1.5 collective-permute-done.1.refs_1_
  110.0 5.8 %row1.1 = (f32[1024,2048]{1,0:T(8,128)S(1)}, f32[1024,2048]{1,0:T(8,128)S(1)}, f32[8,128]{1,0:T(8,128)S(1)}, f32[8,128]{1,0:T(8,128)S(1)}, f32[16,8,128]{2,1,0:T(8,128)S(1)}) custom-call(f32[8,64,256]{2,1,0:T(8,128)S(1)} %all_to_all.65.refs_0_, f32[8,64,256]{2,1,0:T(8,128)S(1)} %collective-permute-done.1.refs_1_, ...), custom_call_target="tpu_custom_call" | custom-call | tf_op jit(solution)/shard_map/row1/pallas_call | solution.py:299
  115.8 8.7 %all_to_all.66.refs_0_ = f32[16,8,128]{2,1,0:T(8,128)S(1)} all-to-all(f32[16,8,128]{2,1,0:T(8,128)S(1)} %get-tuple-element.58), channel_id=1, replica_groups=mesh['dp'=16,'supp'=16] {'dp'}, dimensions={0} | all-to-all | bytes 131072 | tf_op jit(solution)/shard_map/all_to_all | solution.py:333
  124.5 10.2 %col.3 = (f32[8,128]{1,0:T(8,128)S(1)}, f32[16,16,128]{2,1,0:T(8,128)S(1)}) custom-call(f32[16,8,128]{2,1,0:T(8,128)S(1)} %all_to_all.66.refs_0_, f32[8,128]{1,0:T(8,128)S(1)} %get-tuple-element.59.refs_1_, f32[8,128]{1,0:T(8,128)S(1)} %get-tuple-element.60.refs_2_, f32[16,128]{1,0:T(8,128)S(1)} %get-tuple-element.57.refs_3_, ...), custom_call_target="tpu_custom_call" | custom-call | tf_op jit(solution)/shard_map/col/pallas_call | solution.py:299
  134.7 12.2 %all_to_all.67.refs_0_ = f32[16,16,128]{2,1,0:T(8,128)S(1)} all-to-all(f32[16,16,128]{2,1,0:T(8,128)S(1)} %get-tuple-element.63), channel_id=1, replica_groups=mesh['dp'=16,'supp'=16] {'supp'}, dimensions={0} | all-to-all | bytes 262144 | tf_op jit(solution)/shard_map/all_to_all | solution.py:336
  146.9 2.2 %plan.3 = (f32[1024,2048]{1,0:T(8,128)S(1)}, f32[16,128]{1,0:T(8,128)S(1)}, f32[16,8,128]{2,1,0:T(8,128)S(1)}) custom-call(f32[16,16,128]{2,1,0:T(8,128)S(1)} %all_to_all.67.refs_0_, f32[16,128]{1,0:T(8,128)S(1)} %get-tuple-element.46.refs_1_.refs_3_, f32[16,128]{1,0:T(8,128)S(1)} %bitcast.7, f32[16,128]{1,0:T(8,128)S(1)} %get-tuple-element.57.refs_3_, ...), custom_call_target="tpu_custom_call" | custom-call | tf_op jit(solution)/shard_map/plan/pallas_call | solution.py:299
  149.1 10.3 %all_to_all.68.refs_0_ = f32[16,8,128]{2,1,0:T(8,128)S(1)} all-to-all(f32[16,8,128]{2,1,0:T(8,128)S(1)} %get-tuple-element.65), channel_id=1, replica_groups=mesh['dp'=16,'supp'=16] {'dp'}, dimensions={0} | all-to-all | bytes 131072 | tf_op jit(solution)/shard_map/all_to_all | solution.py:333
  159.4 1.1 colsum.3
  160.5 11.9 %all_to_all.69.refs_0_ = f32[16,16,128]{2,1,0:T(8,128)S(1)} all-to-all(f32[16,16,128]{2,1,0:T(8,128)S(1)} %get-tuple-element.67), channel_id=1, replica_groups=mesh['dp'=16,'supp'=16] {'supp'}, dimensions={0} | all-to-all | bytes 262144 | tf_op jit(solution)/shard_map/all_to_all | solution.py:336
  172.4 3.1 %send.3 = (f32[8,136,128]{2,1,0:T(8,128)S(1)}, bf16[6144,256]{1,0:T(8,128)(2,1)S(1)}, f32[16,128]{1,0:T(8,128)S(1)}, f32[16,128]{1,0:T(8,128)}) custom-call(f32[16,16,128]{2,1,0:T(8,128)S(1)} %all_to_all.69.refs_0_, f32[16,128]{1,0:T(8,128)S(1)} %bitcast.8, f32[16,128]{1,0:T(8,128)S(1)} %get-tuple-element.68.refs_2_, ...), custom_call_target="tpu_custom_call" | custom-call | tf_op jit(solution)/shard_map/send/pallas_call | solution.py:299
  175.5 2.0 collective-permute-start.2
  177.5 2.3 %keep.3.refs_0_ = f32[8,136,128]{2,1,0:T(8,128)S(1)} custom-call(f32[16,128]{1,0:T(8,128)S(1)} %get-tuple-element.70.refs_0_, f32[8,128]{1,0:T(8,128)S(1)} %get-tuple-element.69.refs_4_.refs_1_, f32[1024,2048]{1,0:T(8,128)S(1)} %get-tuple-element.66.refs_1_.refs_5_.refs_2_, bf16[6144,256]{1,0:T(8,128)(2,1)S(1)} %get-tuple-element.71.refs_3_), custom_call_target="tpu_custom_call" | custom-call | tf_op jit(solution)/shard_map/keep/pallas_call | solution.py:299
  179.8 0.0 collective-permute-done.2.refs_1_
  179.8 0.1 add.3
  179.9 12.8 %all_to_all.70.refs_0_ = f32[8,136,128]{2,1,0:T(8,128)S(1)} all-to-all(f32[8,136,128]{2,1,0:T(8,128)S(1)} %add.3), channel_id=1, replica_groups={{0,32,64,96,128,160,192,224},{16,48,80,112,144,176,208,240},{1,33,65,97..., dimensions={0} | all-to-all | bytes 1114112 | tf_op jit(solution)/shard_map/all_to_all | solution.py:362
  192.7 0.1 divide.3
  192.9 11.4 %all_to_all.71 = f32[8,64,256]{2,1,0:T(8,128)S(1)} all-to-all(f32[8,64,256]{2,1,0:T(8,128)S(1)} %divide.3), channel_id=1, replica_groups={{0,32,64,96,128,160,192,224},{16,48,80,112,144,176,208,240},{1,33,65,97..., dimensions={0} | all-to-all | bytes 1048576 | tf_op jit(solution)/shard_map/all_to_all | solution.py:364
  204.3 2.0 collective-permute-start.3
  206.3 1.5 collective-permute-done.3
  207.9 1.0 join.1
Async XLA Ops:
  20.0 29.6 %copy-start.1 = (f32[2048]{0:T(1024)S(1)}, f32[2048]{0:T(1024)}, u32[]{:S(2)}) copy-start(f32[2048]{0:T(1024)} %param.5) | copy-start | bytes 24580
  49.6 25.4 %copy-start = (f32[2048,256]{1,0:T(8,128)S(1)}, f32[2048,256]{1,0:T(8,128)}, u32[]{:S(2)}) copy-start(f32[2048,256]{1,0:T(8,128)} %refs_6_.3) | copy-start | bytes 6291460
  77.6 4.4 %collective-permute-start = (f32[8,136,128]{2,1,0:T(8,128)S(1)}, f32[8,136,128]{2,1,0:T(8,128)S(1)}, u32[]{:S(2)}, u32[]{:S(2)}) collective-permute-start(f32[8,136,128]{2,1,0:T(8,128)S(1)} %get-tuple-element.55), channel_id=1, source_target_pairs={{0,16},{16,0},{32,48},{48,32},{64,80},{80,64},{96,112},{112,96},{1... | collective-permute-start | bytes 1671176 | tf_op jit(solution)/shard_map/ppermute | solution.py:359
  106.5 3.6 %collective-permute-start.1 = (f32[8,64,256]{2,1,0:T(8,128)S(1)}, f32[8,64,256]{2,1,0:T(8,128)S(1)}, u32[]{:S(2)}, u32[]{:S(2)}) collective-permute-start(f32[8,64,256]{2,1,0:T(8,128)S(1)} %all_to_all.65.refs_0_), channel_id=1, source_target_pairs={{0,16},{16,0},{32,48},{48,32},{64,80},{80,64},{96,112},{112,96},{1... | collective-permute-start | bytes 1572872 | tf_op jit(solution)/shard_map/ppermute | solution.py:365
  175.5 4.3 %collective-permute-start.2 = (f32[8,136,128]{2,1,0:T(8,128)S(1)}, f32[8,136,128]{2,1,0:T(8,128)S(1)}, u32[]{:S(2)}, u32[]{:S(2)}) collective-permute-start(f32[8,136,128]{2,1,0:T(8,128)S(1)} %get-tuple-element.72), channel_id=1, source_target_pairs={{0,16},{16,0},{32,48},{48,32},{64,80},{80,64},{96,112},{112,96},{1... | collective-permute-start | bytes 1671176 | tf_op jit(solution)/shard_map/ppermute | solution.py:359
  204.3 3.6 %collective-permute-start.3 = (f32[8,64,256]{2,1,0:T(8,128)S(1)}, f32[8,64,256]{2,1,0:T(8,128)S(1)}, u32[]{:S(2)}, u32[]{:S(2)}) collective-permute-start(f32[8,64,256]{2,1,0:T(8,128)S(1)} %all_to_all.71), channel_id=1, source_target_pairs={{0,16},{16,0},{32,48},{48,32},{64,80},{80,64},{96,112},{112,96},{1... | collective-permute-start | bytes 1572872 | tf_op jit(solution)/shard_map/ppermute | solution.py:365

commit v5 on v4

--- a/solution.py
+++ b/solution.py
@@ -65,48 +65,64 @@
         norm_ref[a : a + 1, :] = lane_row(fold(block * block)) * scale
 
 
-def row_step(points_ref, wide_ref, shift_ref, scores_ref, plan_ref, norm_ref, top_ref, out_ref, cols_ref, peak_ref, total_ref, scale):
-    m, n = scores_ref.shape
-    tiles = n // LANES
-    spread_cols(shift_ref, cols_ref)
-    high, low = split(points_ref[...] * (2.0 * scale))
+def score_half(points, wide_ref, cols_ref, put, peak_ref, scale, beside=None):
+    high, low = split(points * (2.0 * scale))
     left = jnp.concatenate([high, low, high], axis=1)
-    for k in range(0, n, 256):
-        acc = lax.dot_general(left, wide_ref[k : k + 256, :], (((1,), (1,)), ((), ())), preferred_element_type=F32)
-        acc = acc + cols_ref[0:1, k : k + 256]
-        scores_ref[:, k : k + 256] = acc
-        best = jnp.maximum(acc[:, :LANES], acc[:, LANES:])
+    for k in range(0, wide_ref.shape[0], 512):
+        acc = lax.dot_general(left, wide_ref[k : k + 512, :], (((1,), (1,)), ((), ())), preferred_element_type=F32)
+        acc = acc + cols_ref[0:1, k : k + 512]
+        put(k, acc)
+        best = tree(jnp.maximum, [acc[:, q : q + LANES] for q in range(0, 512, LANES)])
         peak_ref[...] = best if k == 0 else jnp.maximum(peak_ref[...], best)
-    for a in range(m // LANES):
+        if beside is not None:
+            [beside(k // 256 + q) for q in range(2)]
+
+
+def row_peaks(peak_ref, top_ref):
+    for a in range(peak_ref.shape[0] // LANES):
         rows = slice(a * LANES, (a + 1) * LANES)
         top = jnp.max(peak_ref[rows, :].T, axis=0, keepdims=True)
         top_ref[a : a + 1, :] = top
         peak_ref[rows, :] = jnp.broadcast_to(top, (LANES, LANES)).T
 
+
+def exp_rows(get, peak, plan_ref, rows, total_ref, total_rows):
+    values = []
+    for t in range(plan_ref.shape[1] // LANES):
+        value = jnp.exp2(get(t) - peak)
+        plan_ref[rows, t * LANES : (t + 1) * LANES] = value
+        values.append(value)
+    total_ref[total_rows, :] = tree(jnp.add, values)
+
+
+def tile(t):
+    return slice(t * LANES, (t + 1) * LANES)
+
+
+def exp_loop(scores_ref, base, peak_ref, plan_ref, total_ref):
     def step(b, carry):
-        for half in range(4):
-            rows = pl.ds(pl.multiple_of(b * 32 + half * 8, 8), 8)
-            peak = peak_ref[rows, :]
-            values = []
-            for t in range(tiles):
-                cols = slice(t * LANES, (t + 1) * LANES)
-                value = jnp.exp2(scores_ref[rows, cols] - peak)
-                plan_ref[rows, cols] = value
-                values.append(value)
-            total_ref[rows, :] = tree(jnp.add, values)
+        for part in range(4):
+            at = pl.ds(pl.multiple_of(b * 32 + part * 8, 8), 8)
+            rows = pl.ds(pl.multiple_of(base + b * 32 + part * 8, 8), 8)
+            exp_rows(lambda t: scores_ref[rows, tile(t)], peak_ref[at, :], plan_ref, rows, total_ref, at)
         return carry
 
-    lax.fori_loop(0, m // 32, step, 0)
-    for a in range(m // LANES):
-        rows = slice(a * LANES, (a + 1) * LANES)
-        block = points_ref[rows, :]
-        norm_ref[a : a + 1, :] = lane_row(fold(block * block)) * scale
-        value = top_ref[a : a + 1, :] + jnp.log2(lane_row(total_ref[rows, :]))
+    lax.fori_loop(0, peak_ref.shape[0] // 32, step, 0)
+
+
+def finish_half(points, first, peak_top_ref, total_ref, norm_ref, top_ref, out_ref, scale):
+    for a in range(total_ref.shape[0] // LANES):
+        block = points(a)
+        at = pl.ds(first + a, 1)
+        top = peak_top_ref[a : a + 1, :]
+        norm_ref[at, :] = lane_row(fold(block * block)) * scale
+        top_ref[at, :] = top
+        value = top + jnp.log2(lane_row(total_ref[tile(a), :]))
         for d in range(out_ref.shape[0]):
-            out_ref[d, a : a + 1, :] = value
-
-
-def start_kernel(points_hbm, x_hbm, scores_ref, plan_ref, norm_ref, top_ref, out_ref, wide_ref, col_norm_ref, shift_ref, cols_ref, peak_ref, total_ref, points_ref, x_ref, sems, *, scale):
+            out_ref[d, at, :] = value
+
+
+def start_kernel(points_hbm, x_hbm, scores_ref, plan_ref, norm_ref, top_ref, out_ref, wide_ref, col_norm_ref, shift_ref, cols_ref, peak0_ref, peak1_ref, top0_ref, top1_ref, total0_ref, total1_ref, points_ref, x_ref, sems, *, scale):
     pieces = 4
     count = x_ref.shape[0] // pieces
     copies = [pltpu.make_async_copy(x_hbm.at[k * count : (k + 1) * count], x_ref.at[k * count : (k + 1) * count], sems.at[k]) for k in range(pieces)]
@@ -118,24 +134,73 @@
         prepare(x_ref, wide_ref, col_norm_ref, scale, k * count, count)
     copies[pieces].wait()
     shift_ref[...] = -col_norm_ref[...]
-    row_step(points_ref, wide_ref, shift_ref, scores_ref, plan_ref, norm_ref, top_ref, out_ref, cols_ref, peak_ref, total_ref, scale)
-
-
-def next_row_kernel(own_ref, other_ref, wide_ref, shift_ref, scores_ref, plan_ref, norm_ref, top_ref, out_ref, cols_ref, peak_ref, total_ref, points_ref, *, scale):
-    join(own_ref, other_ref, points_ref)
-    row_step(points_ref, wide_ref, shift_ref, scores_ref, plan_ref, norm_ref, top_ref, out_ref, cols_ref, peak_ref, total_ref, scale)
+    spread_cols(shift_ref, cols_ref)
+    half = points_ref.shape[0] // 2
+    groups = half // 8 // (wide_ref.shape[0] // 256)
+
+    def put(start):
+        def store(k, block):
+            scores_ref[start : start + half, k : k + 512] = block
+
+        return store
+
+    def beside(k):
+        for g in range(k * groups, (k + 1) * groups):
+            rows = slice(g * 8, (g + 1) * 8)
+            exp_rows(lambda t: scores_ref[rows, tile(t)], peak0_ref[rows, :], plan_ref, rows, total0_ref, rows)
+
+    score_half(points_ref[:half, :], wide_ref, cols_ref, put(0), peak0_ref, scale)
+    row_peaks(peak0_ref, top0_ref)
+    score_half(points_ref[half:, :], wide_ref, cols_ref, put(half), peak1_ref, scale, beside)
+    row_peaks(peak1_ref, top1_ref)
+    exp_loop(scores_ref, half, peak1_ref, plan_ref, total1_ref)
+    finish_half(lambda a: points_ref[tile(a), :], 0, top0_ref, total0_ref, norm_ref, top_ref, out_ref, scale)
+    finish_half(lambda a: points_ref[half + a * LANES : half + (a + 1) * LANES, :], half // LANES, top1_ref, total1_ref, norm_ref, top_ref, out_ref, scale)
+
+
+def own_row_kernel(own_ref, wide_ref, shift_ref, scores_ref, peak_ref, top_ref, cols_ref, *, scale):
+    spread_cols(shift_ref, cols_ref)
+
+    def put(k, block):
+        scores_ref[:, k : k + 512] = block
+
+    score_half(own_ref[...], wide_ref, cols_ref, put, peak_ref, scale)
+    row_peaks(peak_ref, top_ref)
+
+
+def other_row_kernel(own_ref, other_ref, wide_ref, shift_ref, own_scores_ref, peak0_ref, top0_ref, scores_ref, plan_ref, norm_ref, top_ref, out_ref, cols_ref, peak1_ref, top1_ref, total0_ref, total1_ref, *, scale):
+    spread_cols(shift_ref, cols_ref)
+    half = own_ref.shape[0]
+    core = core_index()
+    here = pl.multiple_of(core * half, half)
+    there = pl.multiple_of((1 - core) * half, half)
+    groups = half // 8 // (wide_ref.shape[0] // 256)
+
+    def put(k, block):
+        scores_ref[pl.ds(there, half), k : k + 512] = block
+
+    def beside(k):
+        for g in range(k * groups, (k + 1) * groups):
+            rows = slice(g * 8, (g + 1) * 8)
+            at = pl.ds(pl.multiple_of(here + g * 8, 8), 8)
+
+            def get(t):
+                value = own_scores_ref[rows, tile(t)]
+                scores_ref[at, tile(t)] = value
+                return value
+
+            exp_rows(get, peak0_ref[rows, :], plan_ref, at, total0_ref, rows)
+
+    score_half(other_ref[...], wide_ref, cols_ref, put, peak1_ref, scale, beside)
+    row_peaks(peak1_ref, top1_ref)
+    exp_loop(scores_ref, there, peak1_ref, plan_ref, total1_ref)
+    blocks = half // LANES
+    finish_half(lambda a: own_ref[tile(a), :], core * blocks, top0_ref, total0_ref, norm_ref, top_ref, out_ref, scale)
+    finish_half(lambda a: other_ref[tile(a), :], (1 - core) * blocks, top1_ref, total1_ref, norm_ref, top_ref, out_ref, scale)
 
 
 def core_index():
     return lax.axis_index("dp") % 2
-
-
-def join(own_ref, other_ref, points_ref):
-    half = points_ref.shape[0] // 2
-    core = core_index()
-    for d in range(own_ref.shape[0]):
-        points_ref[pl.ds(pl.multiple_of(core * half + d * ROWS, ROWS), ROWS), :] = own_ref[d]
-        points_ref[pl.ds(pl.multiple_of((1 - core) * half + d * ROWS, ROWS), ROWS), :] = other_ref[d]
 
 
 def join_kernel(own_ref, other_ref, points_hbm, sems):
@@ -337,17 +402,21 @@
 
     weight = data_weight.reshape(nr, LANES)
     stack_t = sds((3 * n, dim), BF16)
+    half_s, top_s = pltpu.VMEM((m // 2, LANES), F32), pltpu.VMEM((mr // 2, LANES), F32)
     mass_s = pltpu.VMEM((8, LANES), F32)
     acc_s = pltpu.VMEM((m // 2, dim), F32)
     for update_step in range(OUTER):
         outs = (scores_t, scores_t, row_t, row_t, row_parts_t)
-        scratch = [col_s, row_s, row_s]
         if update_step == 0:
             outs = outs + (sds((n, 3 * dim), BF16), col_t, col_t)
-            scores, raw, row_norm, top, parts, wide_x, col_norm, shift = call(start_kernel, outs, scratch + [pltpu.VMEM((m, dim), F32), pltpu.VMEM((n, dim), F32), pltpu.SemaphoreType.DMA((5,))], "row0", inputs=pltpu.HBM, scale=scale)(*[pltpu.with_memory_space_constraint(v, pltpu.HBM) for v in (support_points, data_points)])
+            scratch = [col_s, half_s, half_s, top_s, top_s, half_s, half_s, pltpu.VMEM((m, dim), F32), pltpu.VMEM((n, dim), F32), pltpu.SemaphoreType.DMA((5,))]
+            held = [pltpu.with_memory_space_constraint(v, pltpu.HBM) for v in (support_points, data_points)]
+            scores, raw, row_norm, top, parts, wide_x, col_norm, shift = call(start_kernel, outs, scratch, "row0", inputs=pltpu.HBM, scale=scale)(*held)
         else:
-            scratch = scratch + [pltpu.VMEM((m, dim), F32)]
-            scores, raw, row_norm, top, parts = call(next_row_kernel, outs, scratch, "row1", scale=scale)(own, other, wide_x, shift)
+            own_outs = (sds((m // 2, n), F32), sds((m // 2, LANES), F32), sds((mr // 2, LANES), F32))
+            early = call(own_row_kernel, own_outs, [col_s], "own", scale=scale)(own, wide_x, shift)
+            scratch = [col_s, half_s, top_s, half_s, half_s]
+            scores, raw, row_norm, top, parts = call(other_row_kernel, outs, scratch, "other", scale=scale)(own, other, wide_x, shift, *early)
         parts = over_dp(parts)
         row_dual, parts = call(first_col_kernel, (row_t, col_parts_t), [row_s, pltpu.VMEM((mr, LANES), F32)], "col", log_support=-math.log2(total))(parts, row_norm, top, shift, scores, raw)
         parts = over_supp(parts)
@@ -362,9 +431,9 @@
         wide = lax.all_to_all(wide, "dp", 0, 0, axis_index_groups=groups)
         own = call(divide_kernel, points_t, [pltpu.VMEM((LANES, LANES), F32)], "divide")(wide)
         own = lax.all_to_all(own, "dp", 0, 0, axis_index_groups=groups)
+        own = own.reshape(m // 2, dim)
         other = lax.ppermute(own, "dp", pairs)
-    halves = (own.reshape(m // 2, dim), other.reshape(m // 2, dim))
-    return call(join_kernel, sds((m, dim), F32), [pltpu.SemaphoreType.DMA((2,))], "join", outputs=pltpu.HBM)(*halves)
+    return call(join_kernel, sds((m, dim), F32), [pltpu.SemaphoreType.DMA((2,))], "join", outputs=pltpu.HBM)(own, other)
 
 
 def solution(mesh):

time: 210 us -> 207 us (0.986)
    pallas_call x17 -> x18, Pallas kernels: 52.1 us -> 51.7 us  [run(): pl.pallas_call(lambda *refs: kernel(*refs, **params), out_shape=outs, in_...]
  transfers between devices with their start and end apart: 4 -> 4, of which waited for: 2 -> 1; matrix products, arithmetic and copies ran while one was open for 0% -> 0% of each run, Pallas kernels for 2% -> 3%
where the time goes in v5:
time: 207 us
  blocking collectives  145 us (70%)
  Pallas kernels  51.7 us (25%)
  starting transfers between devices  8.11 us (4%)
    all_to_all x4, blocking collectives, over_supp(): return lax.all_to_all(parts, 'supp', 0, 0)  55.2 us
    pallas_call x18, Pallas kernels, run(): pl.pallas_call(lambda *refs: kernel(*refs, **params), out_shape=outs, in_...  51.7 us
    all_to_all x4, blocking collectives, over_dp(): return lax.all_to_all(parts, 'dp', 0, 0)  41.4 us
    all_to_all x2, blocking collectives, body(): wide = lax.all_to_all(wide, 'dp', 0, 0, axis_index_groups=groups)  25.6 us
    all_to_all x2, blocking collectives, body(): own = lax.all_to_all(own, 'dp', 0, 0, axis_index_groups=groups)  22.8 us
  transfers between devices with their start and end apart: 4, of which 1 were waited for; matrix products, arithmetic and copies ran while one was open for 0% of the time, Pallas kernels for 3%

profile of v5, /device:TPU:1, one launch (start us, length us, event | category | flops | bytes accessed | tf_op | source)
XLA Modules:
  0.0 206.9 jit_solution(12365436689737336839)
XLA Ops:
  0.0 7.3 %row0.1 = (f32[1024,2048]{1,0:T(8,128)S(1)}, f32[1024,2048]{1,0:T(8,128)S(1)}, f32[8,128]{1,0:T(8,128)S(1)}, f32[8,128]{1,0:T(8,128)S(1)}, f32[16,8,128]{2,1,0:T...) custom-call(f32[1024,256]{1,0:T(8,128)} %refs_0_.1, f32[2048,256]{1,0:T(8,128)} %refs_6_.3), custom_call_target="tpu_custom_call" | custom-call | tf_op jit(solution)/shard_map/row0/pallas_call | solution.py:364
  7.3 12.4 %all_to_all.60.refs_0_ = f32[16,8,128]{2,1,0:T(8,128)S(1)} all-to-all(f32[16,8,128]{2,1,0:T(8,128)S(1)} %get-tuple-element.42), channel_id=1, replica_groups=mesh['dp'=16,'supp'=16] {'dp'}, dimensions={0} | all-to-all | bytes 131072 | tf_op jit(solution)/shard_map/all_to_all | solution.py:398
  19.7 0.0 copy-start.1
  19.7 10.2 %col.2 = (f32[8,128]{1,0:T(8,128)S(1)}, f32[16,16,128]{2,1,0:T(8,128)S(1)}) custom-call(f32[16,8,128]{2,1,0:T(8,128)S(1)} %all_to_all.60.refs_0_, f32[8,128]{1,0:T(8,128)S(1)} %get-tuple-element.43.refs_1_, f32[8,128]{1,0:T(8,128)S(1)} %get-tuple-element.44.refs_2_, f32[16,128]{1,0:T(8,128)S(1)} %get-tuple-element.45.refs_3_, ...), custom_call_target="tpu_custom_call" | custom-call | tf_op jit(solution)/shard_map/col/pallas_call | solution.py:364
  29.9 19.4 %all_to_all.61.refs_0_ = f32[16,16,128]{2,1,0:T(8,128)S(1)} all-to-all(f32[16,16,128]{2,1,0:T(8,128)S(1)} %get-tuple-element.48), channel_id=1, replica_groups=mesh['dp'=16,'supp'=16] {'supp'}, dimensions={0} | all-to-all | bytes 262144 | tf_op jit(solution)/shard_map/all_to_all | solution.py:401
  49.3 0.0 copy-done.1
  49.3 0.0 copy-start
  49.3 2.2 %plan.2 = (f32[1024,2048]{1,0:T(8,128)S(1)}, f32[16,128]{1,0:T(8,128)S(1)}, f32[16,8,128]{2,1,0:T(8,128)S(1)}) custom-call(f32[16,16,128]{2,1,0:T(8,128)S(1)} %all_to_all.61.refs_0_, f32[16,128]{1,0:T(8,128)S(1)} %get-tuple-element.49.refs_1_.refs_3_, f32[16,128]{1,0:T(8,128)S(1)} %bitcast.8, f32[16,128]{1,0:T(8,128)S(1)} %get-tuple-element.45.refs_3_, ...), custom_call_target="tpu_custom_call" | custom-call | tf_op jit(solution)/shard_map/plan/pallas_call | solution.py:364
  51.5 10.3 %all_to_all.62.refs_0_ = f32[16,8,128]{2,1,0:T(8,128)S(1)} all-to-all(f32[16,8,128]{2,1,0:T(8,128)S(1)} %get-tuple-element.51), channel_id=1, replica_groups=mesh['dp'=16,'supp'=16] {'dp'}, dimensions={0} | all-to-all | bytes 131072 | tf_op jit(solution)/shard_map/all_to_all | solution.py:398
  61.8 1.1 colsum.2
  62.9 11.8 %all_to_all.63.refs_0_ = f32[16,16,128]{2,1,0:T(8,128)S(1)} all-to-all(f32[16,16,128]{2,1,0:T(8,128)S(1)} %get-tuple-element.53), channel_id=1, replica_groups=mesh['dp'=16,'supp'=16] {'supp'}, dimensions={0} | all-to-all | bytes 262144 | tf_op jit(solution)/shard_map/all_to_all | solution.py:401
  74.7 0.0 copy-done
  74.7 2.5 %send.2 = (f32[8,136,128]{2,1,0:T(8,128)S(1)}, bf16[6144,256]{1,0:T(8,128)(2,1)S(1)}, f32[16,128]{1,0:T(8,128)S(1)}, f32[16,128]{1,0:T(8,128)S(1)}) custom-call(f32[16,16,128]{2,1,0:T(8,128)S(1)} %all_to_all.63.refs_0_, f32[16,128]{1,0:T(8,128)S(1)} %bitcast.9, f32[16,128]{1,0:T(8,128)S(1)} %get-tuple-element.54.refs_2_, ...), custom_call_target="tpu_custom_call" | custom-call | tf_op jit(solution)/shard_map/send/pallas_call | solution.py:364
  77.2 2.1 collective-permute-start
  79.3 2.4 %keep.2.refs_0_ = f32[8,136,128]{2,1,0:T(8,128)S(1)} custom-call(f32[16,128]{1,0:T(8,128)S(1)} %get-tuple-element.56.refs_0_, f32[8,128]{1,0:T(8,128)S(1)} %get-tuple-element.55.refs_4_.refs_1_, f32[1024,2048]{1,0:T(8,128)S(1)} %get-tuple-element.52.refs_1_.refs_5_.refs_2_, bf16[6144,256]{1,0:T(8,128)(2,1)S(1)} %get-tuple-element.57.refs_3_), custom_call_target="tpu_custom_call" | custom-call | tf_op jit(solution)/shard_map/keep/pallas_call | solution.py:364
  81.7 0.0 collective-permute-done.refs_1_
  81.7 0.1 add.2
  81.7 12.8 %all_to_all.64.refs_0_ = f32[8,136,128]{2,1,0:T(8,128)S(1)} all-to-all(f32[8,136,128]{2,1,0:T(8,128)S(1)} %add.2), channel_id=1, replica_groups={{0,32,64,96,128,160,192,224},{16,48,80,112,144,176,208,240},{1,33,65,97..., dimensions={0} | all-to-all | bytes 1114112 | tf_op jit(solution)/shard_map/all_to_all | solution.py:431
  94.6 0.1 divide.2
  94.7 11.4 %all_to_all.65 = f32[8,64,256]{2,1,0:T(8,128)S(1)} all-to-all(f32[8,64,256]{2,1,0:T(8,128)S(1)} %divide.2), channel_id=1, replica_groups={{0,32,64,96,128,160,192,224},{16,48,80,112,144,176,208,240},{1,33,65,97..., dimensions={0} | all-to-all | bytes 1048576 | tf_op jit(solution)/shard_map/all_to_all | solution.py:433
  106.1 2.0 collective-permute-start.1
  108.1 2.0 own.1
  110.2 0.0 collective-permute-done.1.refs_1_
  110.2 3.7 %other.1 = (f32[1024,2048]{1,0:T(8,128)S(1)}, f32[1024,2048]{1,0:T(8,128)S(1)}, f32[8,128]{1,0:T(8,128)S(1)}, f32[8,128]{1,0:T(8,128)S(1)}, f32[16,8,128]{2,1,0:T(8,128)S(1)}) custom-call(f32[512,256]{1,0:T(8,128)S(1)} %bitcast.5, f32[512,256]{1,0:T(8,128)S(1)} %collective-permute-done.1.refs_1_, bf16[2048,768]{1,0:T(8,128)(2,1)S(1)} %get-tuple-element.59.refs_1_.refs_2_, ...), custom_call_target="tpu_custom_call" | custom-call | tf_op jit(solution)/shard_map/other/pallas_call | solution.py:364
  113.9 8.5 %all_to_all.66.refs_0_ = f32[16,8,128]{2,1,0:T(8,128)S(1)} all-to-all(f32[16,8,128]{2,1,0:T(8,128)S(1)} %get-tuple-element.64), channel_id=1, replica_groups=mesh['dp'=16,'supp'=16] {'dp'}, dimensions={0} | all-to-all | bytes 131072 | tf_op jit(solution)/shard_map/all_to_all | solution.py:398
  122.4 10.2 %col.3 = (f32[8,128]{1,0:T(8,128)S(1)}, f32[16,16,128]{2,1,0:T(8,128)S(1)}) custom-call(f32[16,8,128]{2,1,0:T(8,128)S(1)} %all_to_all.66.refs_0_, f32[8,128]{1,0:T(8,128)S(1)} %get-tuple-element.65.refs_1_, f32[8,128]{1,0:T(8,128)S(1)} %get-tuple-element.66.refs_2_, f32[16,128]{1,0:T(8,128)S(1)} %get-tuple-element.60.refs_2_.refs_3_, ...), custom_call_target="tpu_custom_call" | custom-call | tf_op jit(solution)/shard_map/col/pallas_call | solution.py:364
  132.6 12.2 %all_to_all.67.refs_0_ = f32[16,16,128]{2,1,0:T(8,128)S(1)} all-to-all(f32[16,16,128]{2,1,0:T(8,128)S(1)} %get-tuple-element.69), channel_id=1, replica_groups=mesh['dp'=16,'supp'=16] {'supp'}, dimensions={0} | all-to-all | bytes 262144 | tf_op jit(solution)/shard_map/all_to_all | solution.py:401
  144.7 2.2 %plan.3 = (f32[1024,2048]{1,0:T(8,128)S(1)}, f32[16,128]{1,0:T(8,128)S(1)}, f32[16,8,128]{2,1,0:T(8,128)S(1)}) custom-call(f32[16,16,128]{2,1,0:T(8,128)S(1)} %all_to_all.67.refs_0_, f32[16,128]{1,0:T(8,128)S(1)} %get-tuple-element.49.refs_1_.refs_3_, f32[16,128]{1,0:T(8,128)S(1)} %bitcast.10, f32[16,128]{1,0:T(8,128)S(1)} %get-tuple-element.60.refs_2_.refs_3_, ...), custom_call_target="tpu_custom_call" | custom-call | tf_op jit(solution)/shard_map/plan/pallas_call | solution.py:364
  147.0 10.3 %all_to_all.68.refs_0_ = f32[16,8,128]{2,1,0:T(8,128)S(1)} all-to-all(f32[16,8,128]{2,1,0:T(8,128)S(1)} %get-tuple-element.71), channel_id=1, replica_groups=mesh['dp'=16,'supp'=16] {'dp'}, dimensions={0} | all-to-all | bytes 131072 | tf_op jit(solution)/shard_map/all_to_all | solution.py:398
  157.3 1.1 colsum.3
  158.3 11.9 %all_to_all.69.refs_0_ = f32[16,16,128]{2,1,0:T(8,128)S(1)} all-to-all(f32[16,16,128]{2,1,0:T(8,128)S(1)} %get-tuple-element.73), channel_id=1, replica_groups=mesh['dp'=16,'supp'=16] {'supp'}, dimensions={0} | all-to-all | bytes 262144 | tf_op jit(solution)/shard_map/all_to_all | solution.py:401
  170.2 3.1 %send.3 = (f32[8,136,128]{2,1,0:T(8,128)S(1)}, bf16[6144,256]{1,0:T(8,128)(2,1)S(1)}, f32[16,128]{1,0:T(8,128)S(1)}, f32[16,128]{1,0:T(8,128)}) custom-call(f32[16,16,128]{2,1,0:T(8,128)S(1)} %all_to_all.69.refs_0_, f32[16,128]{1,0:T(8,128)S(1)} %bitcast.11, f32[16,128]{1,0:T(8,128)S(1)} %get-tuple-element.74.refs_2_, ...), custom_call_target="tpu_custom_call" | custom-call | tf_op jit(solution)/shard_map/send/pallas_call | solution.py:364
  173.3 2.0 collective-permute-start.2
  175.3 2.4 %keep.3.refs_0_ = f32[8,136,128]{2,1,0:T(8,128)S(1)} custom-call(f32[16,128]{1,0:T(8,128)S(1)} %get-tuple-element.76.refs_0_, f32[8,128]{1,0:T(8,128)S(1)} %get-tuple-element.75.refs_4_.refs_1_, f32[1024,2048]{1,0:T(8,128)S(1)} %get-tuple-element.72.refs_1_.refs_5_.refs_2_, bf16[6144,256]{1,0:T(8,128)(2,1)S(1)} %get-tuple-element.77.refs_3_), custom_call_target="tpu_custom_call" | custom-call | tf_op jit(solution)/shard_map/keep/pallas_call | solution.py:364
  177.7 0.0 collective-permute-done.2.refs_1_
  177.7 0.1 add.3
  177.8 12.8 %all_to_all.70.refs_0_ = f32[8,136,128]{2,1,0:T(8,128)S(1)} all-to-all(f32[8,136,128]{2,1,0:T(8,128)S(1)} %add.3), channel_id=1, replica_groups={{0,32,64,96,128,160,192,224},{16,48,80,112,144,176,208,240},{1,33,65,97..., dimensions={0} | all-to-all | bytes 1114112 | tf_op jit(solution)/shard_map/all_to_all | solution.py:431
  190.6 0.1 divide.3
  190.7 11.4 %all_to_all.71 = f32[8,64,256]{2,1,0:T(8,128)S(1)} all-to-all(f32[8,64,256]{2,1,0:T(8,128)S(1)} %divide.3), channel_id=1, replica_groups={{0,32,64,96,128,160,192,224},{16,48,80,112,144,176,208,240},{1,33,65,97..., dimensions={0} | all-to-all | bytes 1048576 | tf_op jit(solution)/shard_map/all_to_all | solution.py:433
  202.1 2.0 collective-permute-start.3
  204.2 1.5 collective-permute-done.3.refs_1_
  205.7 1.0 join.1
Async XLA Ops:
  19.7 29.6 %copy-start.1 = (f32[2048]{0:T(1024)S(1)}, f32[2048]{0:T(1024)}, u32[]{:S(2)}) copy-start(f32[2048]{0:T(1024)} %param.5) | copy-start | bytes 24580
  49.3 25.4 %copy-start = (f32[2048,256]{1,0:T(8,128)S(1)}, f32[2048,256]{1,0:T(8,128)}, u32[]{:S(2)}) copy-start(f32[2048,256]{1,0:T(8,128)} %refs_6_.3) | copy-start | bytes 6291460
  77.2 4.5 %collective-permute-start = (f32[8,136,128]{2,1,0:T(8,128)S(1)}, f32[8,136,128]{2,1,0:T(8,128)S(1)}, u32[]{:S(2)}, u32[]{:S(2)}) collective-permute-start(f32[8,136,128]{2,1,0:T(8,128)S(1)} %get-tuple-element.58), channel_id=1, source_target_pairs={{0,16},{16,0},{32,48},{48,32},{64,80},{80,64},{96,112},{112,96},{1... | collective-permute-start | bytes 1671176 | tf_op jit(solution)/shard_map/ppermute | solution.py:428
  106.1 4.0 %collective-permute-start.1 = (f32[512,256]{1,0:T(8,128)S(1)}, f32[512,256]{1,0:T(8,128)S(1)}, u32[]{:S(2)}, u32[]{:S(2)}) collective-permute-start(f32[512,256]{1,0:T(8,128)S(1)} %bitcast.3), channel_id=1, source_target_pairs={{0,16},{16,0},{32,48},{48,32},{64,80},{80,64},{96,112},{112,96},{1... | collective-permute-start | bytes 1572872 | tf_op jit(solution)/shard_map/ppermute | solution.py:435
  173.3 4.4 %collective-permute-start.2 = (f32[8,136,128]{2,1,0:T(8,128)S(1)}, f32[8,136,128]{2,1,0:T(8,128)S(1)}, u32[]{:S(2)}, u32[]{:S(2)}) collective-permute-start(f32[8,136,128]{2,1,0:T(8,128)S(1)} %get-tuple-element.78), channel_id=1, source_target_pairs={{0,16},{16,0},{32,48},{48,32},{64,80},{80,64},{96,112},{112,96},{1... | collective-permute-start | bytes 1671176 | tf_op jit(solution)/shard_map/ppermute | solution.py:428
  202.1 3.6 %collective-permute-start.3 = (f32[512,256]{1,0:T(8,128)S(1)}, f32[512,256]{1,0:T(8,128)S(1)}, u32[]{:S(2)}, u32[]{:S(2)}) collective-permute-start(f32[512,256]{1,0:T(8,128)S(1)} %bitcast.6), channel_id=1, source_target_pairs={{0,16},{16,0},{32,48},{48,32},{64,80},{80,64},{96,112},{112,96},{1... | collective-permute-start | bytes 1572872 | tf_op jit(solution)/shard_map/ppermute | solution.py:435

commit v6 on v5

--- a/solution.py
+++ b/solution.py
@@ -122,7 +122,7 @@
             out_ref[d, at, :] = value
 
 
-def start_kernel(points_hbm, x_hbm, scores_ref, plan_ref, norm_ref, top_ref, out_ref, wide_ref, col_norm_ref, shift_ref, cols_ref, peak0_ref, peak1_ref, top0_ref, top1_ref, total0_ref, total1_ref, points_ref, x_ref, sems, *, scale):
+def start_kernel(points_hbm, x_hbm, scores_ref, plan_ref, norm_ref, top_ref, out_ref, wide_ref, col_norm_ref, shift_ref, x_ref, cols_ref, peak0_ref, peak1_ref, top0_ref, top1_ref, total0_ref, total1_ref, points_ref, sems, *, scale):
     pieces = 4
     count = x_ref.shape[0] // pieces
     copies = [pltpu.make_async_copy(x_hbm.at[k * count : (k + 1) * count], x_ref.at[k * count : (k + 1) * count], sems.at[k]) for k in range(pieces)]
@@ -408,10 +408,10 @@
     for update_step in range(OUTER):
         outs = (scores_t, scores_t, row_t, row_t, row_parts_t)
         if update_step == 0:
-            outs = outs + (sds((n, 3 * dim), BF16), col_t, col_t)
-            scratch = [col_s, half_s, half_s, top_s, top_s, half_s, half_s, pltpu.VMEM((m, dim), F32), pltpu.VMEM((n, dim), F32), pltpu.SemaphoreType.DMA((5,))]
+            outs = outs + (sds((n, 3 * dim), BF16), col_t, col_t, sds((n, dim), F32))
+            scratch = [col_s, half_s, half_s, top_s, top_s, half_s, half_s, pltpu.VMEM((m, dim), F32), pltpu.SemaphoreType.DMA((5,))]
             held = [pltpu.with_memory_space_constraint(v, pltpu.HBM) for v in (support_points, data_points)]
-            scores, raw, row_norm, top, parts, wide_x, col_norm, shift = call(start_kernel, outs, scratch, "row0", inputs=pltpu.HBM, scale=scale)(*held)
+            scores, raw, row_norm, top, parts, wide_x, col_norm, shift, data = call(start_kernel, outs, scratch, "row0", inputs=pltpu.HBM, scale=scale)(*held)
         else:
             own_outs = (sds((m // 2, n), F32), sds((m // 2, LANES), F32), sds((mr // 2, LANES), F32))
             early = call(own_row_kernel, own_outs, [col_s], "own", scale=scale)(own, wide_x, shift)
@@ -424,7 +424,7 @@
         parts = over_dp(parts)
         factor, parts = call(next_col_sum_kernel, (row_t, col_parts_t), [row_s], "colsum", share=1.0 / total)(parts, plan)
         parts = over_supp(parts)
-        send, stack, ratio, shift = call(send_kernel, (wide_t, stack_t, col_t, col_t), [row_s, mass_s, acc_s], "send")(parts, weight, col_dual, col_norm, factor, plan, data_points)
+        send, stack, ratio, shift = call(send_kernel, (wide_t, stack_t, col_t, col_t), [row_s, mass_s, acc_s], "send")(parts, weight, col_dual, col_norm, factor, plan, data)
         got = lax.ppermute(send, "dp", pairs)
         wide = call(keep_kernel, wide_t, [row_s, mass_s, acc_s], "keep")(ratio, factor, plan, stack)
         wide = call(add_kernel, wide_t, [], "add")(wide, got)

time: 207 us -> 207 us (level)
  no operation moved by 1% of the time
where the time goes in v6:
time: 207 us
  blocking collectives  145 us (70%)
  Pallas kernels  51.8 us (25%)
  starting transfers between devices  8.1 us (4%)
    all_to_all x4, blocking collectives, over_supp(): return lax.all_to_all(parts, 'supp', 0, 0)  55.2 us
    pallas_call x18, Pallas kernels, run(): pl.pallas_call(lambda *refs: kernel(*refs, **params), out_shape=outs, in_...  51.8 us
    all_to_all x4, blocking collectives, over_dp(): return lax.all_to_all(parts, 'dp', 0, 0)  41.5 us
    all_to_all x2, blocking collectives, body(): wide = lax.all_to_all(wide, 'dp', 0, 0, axis_index_groups=groups)  25.6 us
    all_to_all x2, blocking collectives, body(): own = lax.all_to_all(own, 'dp', 0, 0, axis_index_groups=groups)  22.9 us
  transfers between devices with their start and end apart: 4, of which 1 were waited for; matrix products, arithmetic and copies ran while one was open for 0% of the time, Pallas kernels for 3%

profile of v6, /device:TPU:1, one launch (start us, length us, event | category | flops | bytes accessed | tf_op | source)
XLA Modules:
  0.0 206.9 jit_solution(17510080947001644104)
XLA Ops:
  0.0 7.3 %row0.1 = (f32[1024,2048]{1,0:T(8,128)S(1)}, f32[1024,2048]{1,0:T(8,128)S(1)}, f32[8,128]{1,0:T(8,128)S(1)}, f32[8,128]{1,0:T(8,128)S(1)}, f32[16,8,128]{2,1,0:T...) custom-call(f32[1024,256]{1,0:T(8,128)} %refs_0_.1, ...), custom_call_target="tpu_custom_call" | custom-call | tf_op jit(solution)/shard_map/row0/pallas_call | solution.py:364
  7.3 12.4 %all_to_all.60.refs_0_ = f32[16,8,128]{2,1,0:T(8,128)S(1)} all-to-all(f32[16,8,128]{2,1,0:T(8,128)S(1)} %get-tuple-element.43), channel_id=1, replica_groups=mesh['dp'=16,'supp'=16] {'dp'}, dimensions={0} | all-to-all | bytes 131072 | tf_op jit(solution)/shard_map/all_to_all | solution.py:398
  19.7 0.0 copy-start
  19.7 10.2 %col.2 = (f32[8,128]{1,0:T(8,128)S(1)}, f32[16,16,128]{2,1,0:T(8,128)S(1)}) custom-call(f32[16,8,128]{2,1,0:T(8,128)S(1)} %all_to_all.60.refs_0_, f32[8,128]{1,0:T(8,128)S(1)} %get-tuple-element.44.refs_1_, f32[8,128]{1,0:T(8,128)S(1)} %get-tuple-element.45.refs_2_, f32[16,128]{1,0:T(8,128)S(1)} %get-tuple-element.46.refs_3_, ...), custom_call_target="tpu_custom_call" | custom-call | tf_op jit(solution)/shard_map/col/pallas_call | solution.py:364
  29.9 19.4 %all_to_all.61.refs_0_ = f32[16,16,128]{2,1,0:T(8,128)S(1)} all-to-all(f32[16,16,128]{2,1,0:T(8,128)S(1)} %get-tuple-element.49), channel_id=1, replica_groups=mesh['dp'=16,'supp'=16] {'supp'}, dimensions={0} | all-to-all | bytes 262144 | tf_op jit(solution)/shard_map/all_to_all | solution.py:401
  49.3 0.0 copy-done
  49.3 2.2 %plan.2 = (f32[1024,2048]{1,0:T(8,128)S(1)}, f32[16,128]{1,0:T(8,128)S(1)}, f32[16,8,128]{2,1,0:T(8,128)S(1)}) custom-call(f32[16,16,128]{2,1,0:T(8,128)S(1)} %all_to_all.61.refs_0_, f32[16,128]{1,0:T(8,128)S(1)} %get-tuple-element.50.refs_1_.refs_3_, f32[16,128]{1,0:T(8,128)S(1)} %bitcast.8, f32[16,128]{1,0:T(8,128)S(1)} %get-tuple-element.46.refs_3_, ...), custom_call_target="tpu_custom_call" | custom-call | tf_op jit(solution)/shard_map/plan/pallas_call | solution.py:364
  51.5 10.3 %all_to_all.62.refs_0_ = f32[16,8,128]{2,1,0:T(8,128)S(1)} all-to-all(f32[16,8,128]{2,1,0:T(8,128)S(1)} %get-tuple-element.52), channel_id=1, replica_groups=mesh['dp'=16,'supp'=16] {'dp'}, dimensions={0} | all-to-all | bytes 131072 | tf_op jit(solution)/shard_map/all_to_all | solution.py:398
  61.8 1.1 colsum.2
  62.9 11.8 %all_to_all.63.refs_0_ = f32[16,16,128]{2,1,0:T(8,128)S(1)} all-to-all(f32[16,16,128]{2,1,0:T(8,128)S(1)} %get-tuple-element.54), channel_id=1, replica_groups=mesh['dp'=16,'supp'=16] {'supp'}, dimensions={0} | all-to-all | bytes 262144 | tf_op jit(solution)/shard_map/all_to_all | solution.py:401
  74.7 2.6 %send.2 = (f32[8,136,128]{2,1,0:T(8,128)S(1)}, bf16[6144,256]{1,0:T(8,128)(2,1)S(1)}, f32[16,128]{1,0:T(8,128)S(1)}, f32[16,128]{1,0:T(8,128)S(1)}) custom-call(f32[16,16,128]{2,1,0:T(8,128)S(1)} %all_to_all.63.refs_0_, f32[16,128]{1,0:T(8,128)S(1)} %bitcast.9, f32[16,128]{1,0:T(8,128)S(1)} %get-tuple-element.55.refs_2_, ...), custom_call_target="tpu_custom_call" | custom-call | tf_op jit(solution)/shard_map/send/pallas_call | solution.py:364
  77.2 2.1 collective-permute-start
  79.3 2.4 %keep.2.refs_0_ = f32[8,136,128]{2,1,0:T(8,128)S(1)} custom-call(f32[16,128]{1,0:T(8,128)S(1)} %get-tuple-element.58.refs_0_, f32[8,128]{1,0:T(8,128)S(1)} %get-tuple-element.56.refs_4_.refs_1_, f32[1024,2048]{1,0:T(8,128)S(1)} %get-tuple-element.53.refs_1_.refs_5_.refs_2_, bf16[6144,256]{1,0:T(8,128)(2,1)S(1)} %get-tuple-element.59.refs_3_), custom_call_target="tpu_custom_call" | custom-call | tf_op jit(solution)/shard_map/keep/pallas_call | solution.py:364
  81.7 0.0 collective-permute-done.refs_1_
  81.7 0.1 add.2
  81.8 12.8 %all_to_all.64.refs_0_ = f32[8,136,128]{2,1,0:T(8,128)S(1)} all-to-all(f32[8,136,128]{2,1,0:T(8,128)S(1)} %add.2), channel_id=1, replica_groups={{0,32,64,96,128,160,192,224},{16,48,80,112,144,176,208,240},{1,33,65,97..., dimensions={0} | all-to-all | bytes 1114112 | tf_op jit(solution)/shard_map/all_to_all | solution.py:431
  94.6 0.1 divide.2
  94.7 11.4 %all_to_all.65 = f32[8,64,256]{2,1,0:T(8,128)S(1)} all-to-all(f32[8,64,256]{2,1,0:T(8,128)S(1)} %divide.2), channel_id=1, replica_groups={{0,32,64,96,128,160,192,224},{16,48,80,112,144,176,208,240},{1,33,65,97..., dimensions={0} | all-to-all | bytes 1048576 | tf_op jit(solution)/shard_map/all_to_all | solution.py:433
  106.2 2.0 collective-permute-start.1
  108.2 2.0 own.1
  110.2 0.0 collective-permute-done.1.refs_1_
  110.2 3.7 %other.1 = (f32[1024,2048]{1,0:T(8,128)S(1)}, f32[1024,2048]{1,0:T(8,128)S(1)}, f32[8,128]{1,0:T(8,128)S(1)}, f32[8,128]{1,0:T(8,128)S(1)}, f32[16,8,128]{2,1,0:T(8,128)S(1)}) custom-call(f32[512,256]{1,0:T(8,128)S(1)} %bitcast.5, f32[512,256]{1,0:T(8,128)S(1)} %collective-permute-done.1.refs_1_, bf16[2048,768]{1,0:T(8,128)(2,1)S(1)} %get-tuple-element.61.refs_1_.refs_2_, ...), custom_call_target="tpu_custom_call" | custom-call | tf_op jit(solution)/shard_map/other/pallas_call | solution.py:364
  114.0 8.5 %all_to_all.66.refs_0_ = f32[16,8,128]{2,1,0:T(8,128)S(1)} all-to-all(f32[16,8,128]{2,1,0:T(8,128)S(1)} %get-tuple-element.66), channel_id=1, replica_groups=mesh['dp'=16,'supp'=16] {'dp'}, dimensions={0} | all-to-all | bytes 131072 | tf_op jit(solution)/shard_map/all_to_all | solution.py:398
  122.4 10.2 %col.3 = (f32[8,128]{1,0:T(8,128)S(1)}, f32[16,16,128]{2,1,0:T(8,128)S(1)}) custom-call(f32[16,8,128]{2,1,0:T(8,128)S(1)} %all_to_all.66.refs_0_, f32[8,128]{1,0:T(8,128)S(1)} %get-tuple-element.67.refs_1_, f32[8,128]{1,0:T(8,128)S(1)} %get-tuple-element.68.refs_2_, f32[16,128]{1,0:T(8,128)S(1)} %get-tuple-element.62.refs_2_.refs_3_, ...), custom_call_target="tpu_custom_call" | custom-call | tf_op jit(solution)/shard_map/col/pallas_call | solution.py:364
  132.6 12.1 %all_to_all.67.refs_0_ = f32[16,16,128]{2,1,0:T(8,128)S(1)} all-to-all(f32[16,16,128]{2,1,0:T(8,128)S(1)} %get-tuple-element.71), channel_id=1, replica_groups=mesh['dp'=16,'supp'=16] {'supp'}, dimensions={0} | all-to-all | bytes 262144 | tf_op jit(solution)/shard_map/all_to_all | solution.py:401
  144.8 2.2 %plan.3 = (f32[1024,2048]{1,0:T(8,128)S(1)}, f32[16,128]{1,0:T(8,128)S(1)}, f32[16,8,128]{2,1,0:T(8,128)S(1)}) custom-call(f32[16,16,128]{2,1,0:T(8,128)S(1)} %all_to_all.67.refs_0_, f32[16,128]{1,0:T(8,128)S(1)} %get-tuple-element.50.refs_1_.refs_3_, f32[16,128]{1,0:T(8,128)S(1)} %bitcast.10, f32[16,128]{1,0:T(8,128)S(1)} %get-tuple-element.62.refs_2_.refs_3_, ...), custom_call_target="tpu_custom_call" | custom-call | tf_op jit(solution)/shard_map/plan/pallas_call | solution.py:364
  147.0 10.3 %all_to_all.68.refs_0_ = f32[16,8,128]{2,1,0:T(8,128)S(1)} all-to-all(f32[16,8,128]{2,1,0:T(8,128)S(1)} %get-tuple-element.73), channel_id=1, replica_groups=mesh['dp'=16,'supp'=16] {'dp'}, dimensions={0} | all-to-all | bytes 131072 | tf_op jit(solution)/shard_map/all_to_all | solution.py:398
  157.3 1.1 colsum.3
  158.4 11.9 %all_to_all.69.refs_0_ = f32[16,16,128]{2,1,0:T(8,128)S(1)} all-to-all(f32[16,16,128]{2,1,0:T(8,128)S(1)} %get-tuple-element.75), channel_id=1, replica_groups=mesh['dp'=16,'supp'=16] {'supp'}, dimensions={0} | all-to-all | bytes 262144 | tf_op jit(solution)/shard_map/all_to_all | solution.py:401
  170.3 3.1 %send.3 = (f32[8,136,128]{2,1,0:T(8,128)S(1)}, bf16[6144,256]{1,0:T(8,128)(2,1)S(1)}, f32[16,128]{1,0:T(8,128)S(1)}, f32[16,128]{1,0:T(8,128)}) custom-call(f32[16,16,128]{2,1,0:T(8,128)S(1)} %all_to_all.69.refs_0_, f32[16,128]{1,0:T(8,128)S(1)} %bitcast.11, f32[16,128]{1,0:T(8,128)S(1)} %get-tuple-element.76.refs_2_, ...), custom_call_target="tpu_custom_call" | custom-call | tf_op jit(solution)/shard_map/send/pallas_call | solution.py:364
  173.4 2.0 collective-permute-start.2
  175.4 2.4 %keep.3.refs_0_ = f32[8,136,128]{2,1,0:T(8,128)S(1)} custom-call(f32[16,128]{1,0:T(8,128)S(1)} %get-tuple-element.78.refs_0_, f32[8,128]{1,0:T(8,128)S(1)} %get-tuple-element.77.refs_4_.refs_1_, f32[1024,2048]{1,0:T(8,128)S(1)} %get-tuple-element.74.refs_1_.refs_5_.refs_2_, bf16[6144,256]{1,0:T(8,128)(2,1)S(1)} %get-tuple-element.79.refs_3_), custom_call_target="tpu_custom_call" | custom-call | tf_op jit(solution)/shard_map/keep/pallas_call | solution.py:364
  177.8 0.0 collective-permute-done.2.refs_1_
  177.8 0.1 add.3
  177.9 12.8 %all_to_all.70.refs_0_ = f32[8,136,128]{2,1,0:T(8,128)S(1)} all-to-all(f32[8,136,128]{2,1,0:T(8,128)S(1)} %add.3), channel_id=1, replica_groups={{0,32,64,96,128,160,192,224},{16,48,80,112,144,176,208,240},{1,33,65,97..., dimensions={0} | all-to-all | bytes 1114112 | tf_op jit(solution)/shard_map/all_to_all | solution.py:431
  190.7 0.1 divide.3
  190.8 11.4 %all_to_all.71 = f32[8,64,256]{2,1,0:T(8,128)S(1)} all-to-all(f32[8,64,256]{2,1,0:T(8,128)S(1)} %divide.3), channel_id=1, replica_groups={{0,32,64,96,128,160,192,224},{16,48,80,112,144,176,208,240},{1,33,65,97..., dimensions={0} | all-to-all | bytes 1048576 | tf_op jit(solution)/shard_map/all_to_all | solution.py:433
  202.2 2.0 collective-permute-start.3
  204.3 1.5 collective-permute-done.3.refs_1_
  205.8 1.0 join.1
Async XLA Ops:
  19.7 29.6 %copy-start = (f32[2048]{0:T(1024)S(1)}, f32[2048]{0:T(1024)}, u32[]{:S(2)}) copy-start(f32[2048]{0:T(1024)} %param.5) | copy-start | bytes 24580
  77.2 4.5 %collective-permute-start = (f32[8,136,128]{2,1,0:T(8,128)S(1)}, f32[8,136,128]{2,1,0:T(8,128)S(1)}, u32[]{:S(2)}, u32[]{:S(2)}) collective-permute-start(f32[8,136,128]{2,1,0:T(8,128)S(1)} %get-tuple-element.60), channel_id=1, source_target_pairs={{0,16},{16,0},{32,48},{48,32},{64,80},{80,64},{96,112},{112,96},{1... | collective-permute-start | bytes 1671176 | tf_op jit(solution)/shard_map/ppermute | solution.py:428
  106.2 4.0 %collective-permute-start.1 = (f32[512,256]{1,0:T(8,128)S(1)}, f32[512,256]{1,0:T(8,128)S(1)}, u32[]{:S(2)}, u32[]{:S(2)}) collective-permute-start(f32[512,256]{1,0:T(8,128)S(1)} %bitcast.3), channel_id=1, source_target_pairs={{0,16},{16,0},{32,48},{48,32},{64,80},{80,64},{96,112},{112,96},{1... | collective-permute-start | bytes 1572872 | tf_op jit(solution)/shard_map/ppermute | solution.py:435
  173.4 4.4 %collective-permute-start.2 = (f32[8,136,128]{2,1,0:T(8,128)S(1)}, f32[8,136,128]{2,1,0:T(8,128)S(1)}, u32[]{:S(2)}, u32[]{:S(2)}) collective-permute-start(f32[8,136,128]{2,1,0:T(8,128)S(1)} %get-tuple-element.80), channel_id=1, source_target_pairs={{0,16},{16,0},{32,48},{48,32},{64,80},{80,64},{96,112},{112,96},{1... | collective-permute-start | bytes 1671176 | tf_op jit(solution)/shard_map/ppermute | solution.py:428
  202.2 3.6 %collective-permute-start.3 = (f32[512,256]{1,0:T(8,128)S(1)}, f32[512,256]{1,0:T(8,128)S(1)}, u32[]{:S(2)}, u32[]{:S(2)}) collective-permute-start(f32[512,256]{1,0:T(8,128)S(1)} %bitcast.6), channel_id=1, source_target_pairs={{0,16},{16,0},{32,48},{48,32},{64,80},{80,64},{96,112},{112,96},{1... | collective-permute-start | bytes 1572872 | tf_op jit(solution)/shard_map/ppermute | solution.py:435
